TPU v7x, 512 devices: a whole 4x8x8 slice. The times are simulated.
512 devices in a mesh: head: 32 (over x, z), seq: 16 (over y, core).
Axes of the slice: x: 4, y: 8, z: 8, core: 2. Of those that a mesh axis runs over, the one named last changes fastest.
Arguments:
- queries: bfloat16 [16, 4096, 4096], P('seq', 'head'), may hold values from -8 to 8
- key_row_matrix: bfloat16 [16, 4096, 1024], P('seq', 'head'), may hold values from -8 to 8
- values: bfloat16 [16, 4096, 1024], P('seq', 'head'), may hold values from -6 to 6
- verticals: int32 [32, 6], replicated, may hold values from 0 to 511, as said below
- slashes: int32 [32, 3], replicated, may hold values from 1 to 31, as said below
- counts: int32 [32, 2], replicated, may hold values from 0 to 6, as said below
Outputs:
- context: bfloat16 [16, 4096, 4096], P('seq', 'head')
Inputs may be any that keep to these rules, and one draw needn't show every extreme that they name: `verticals`: each row holds 6 different key blocks. `slashes`: each row holds 3 different block offsets. `counts`: column 0 is at least 1; some head uses all 6 and all 3 slots.
All inputs are finite; a program needn't handle non-finite values.
Results may differ from a plain program's by a relative error of at most 0.0037.
Values may be sent and summed in bfloat16 or wider, within the bound.
No kernel may reach another device: no remote copies, remote signals or barrier semaphores. Data moves between devices by JAX's collectives and lax.ppermute only.
A program may use at most 64 MiB of HBM per device.

v0:
```python
import math

import jax
import jax.numpy as jnp
from jax import lax
from jax.experimental import pallas as pl
from jax.experimental.pallas import tpu as pltpu
from jax.sharding import Mesh
from jax.sharding import PartitionSpec as P


QUERY_HEADS = 32
KEY_VALUE_HEADS = 8
HEAD_WIDTH = 128
BLOCK_TOKENS = 128
X_CHIPS = 4
Z_CHIPS = 8
SEGMENTS = 16
NV = 6
NS = 3
SLOTS = 1 + NS + NV
ROW_BLOCKS = 8
SEG_BLOCKS = 32
COLUMN_BASE = 2 * SEG_BLOCKS
POOL_BLOCKS = COLUMN_BASE + NV
GROUP = 4


def shifted(value, axis, distance, size, wrap):
    pairs = [(i, (i + distance) % size) for i in range(size) if wrap or i + distance < size]
    return lax.ppermute(value, axis, pairs)


PART_STARTS = (0, 8, 16, 20, 24)
PART_SIZES = (8, 8, 4, 4, 8)


def column_kernel(place_ref, *refs):
    parts = refs[: len(PART_SIZES)]
    out_ref, sems = refs[len(PART_SIZES) :]
    out_ref[...] = jnp.zeros_like(out_ref)
    for slot in range(NV):
        place = place_ref[slot]
        for part, low, size in zip(parts, PART_STARTS, PART_SIZES):

            @pl.when((place >= low) & (place < low + size))
            def _():
                copy = pltpu.make_async_copy(
                    part.at[place - low], out_ref.at[slot], sems.at[slot]
                )
                copy.start()
                copy.wait()


def own_columns(place, rows):
    return pl.pallas_call(
        column_kernel,
        out_shape=jax.ShapeDtypeStruct((NV, 2, BLOCK_TOKENS, HEAD_WIDTH), jnp.bfloat16),
        grid_spec=pltpu.PrefetchScalarGridSpec(
            num_scalar_prefetch=1,
            grid=(1,),
            in_specs=[pl.BlockSpec(memory_space=pl.ANY)] * len(PART_SIZES),
            out_specs=pl.BlockSpec(
                (NV, 2, BLOCK_TOKENS, HEAD_WIDTH), lambda i, place_ref: (0, 0, 0, 0)
            ),
            scratch_shapes=[pltpu.SemaphoreType.DMA((NV,))],
        ),
        name="own_columns",
    )(place, *rows)


def attention_kernel(
    index_ref, bias_ref, pairs_ref, query_ref, *rest
):
    count = 2 * len(PART_SIZES)
    parts = rest[:count]
    columns, out_ref, pool, score_ref, top_ref, total_ref, mix_ref, sems = rest[count:]
    starts = PART_STARTS + tuple(SEG_BLOCKS + start for start in PART_STARTS)
    copies = [
        pltpu.make_async_copy(part, pool.at[pl.ds(start, size)], sems.at[at])
        for at, (part, start, size) in enumerate(zip(parts, starts, PART_SIZES * 2))
    ]
    copies.append(
        pltpu.make_async_copy(columns, pool.at[pl.ds(COLUMN_BASE, NV)], sems.at[count])
    )
    for copy in copies:
        copy.start()
    for copy in copies:
        copy.wait()
    scale = math.log2(math.e) / math.sqrt(HEAD_WIDTH)
    pairs = pairs_ref[0]
    row_ids = lax.broadcasted_iota(jnp.int32, (BLOCK_TOKENS, BLOCK_TOKENS), 0)
    col_ids = lax.broadcasted_iota(jnp.int32, (BLOCK_TOKENS, BLOCK_TOKENS), 1)
    causal_bias = jnp.where(row_ids >= col_ids, 0.0, -jnp.inf)

    def keys_of(slot, block, part):
        return pool[index_ref[slot, block], part]

    def score(pair, group, first):
        for at in range(GROUP):
            block = group * GROUP + at
            key_pair = jnp.concatenate(
                [keys_of(2 * pair, block, 0), keys_of(2 * pair + 1, block, 0)], axis=0
            )
            found = lax.dot_general(
                query_ref[block],
                key_pair,
                (((1,), (1,)), ((), ())),
                preferred_element_type=jnp.float32,
            )
            left = found[:, :BLOCK_TOKENS]
            right = found[:, BLOCK_TOKENS:] + bias_ref[2 * pair + 1, block]
            if first:
                left = left + causal_bias
                top_ref[at] = jnp.maximum(left, right)
            else:
                left = left + bias_ref[2 * pair, block]
                top_ref[at] = jnp.maximum(top_ref[at], jnp.maximum(left, right))
            score_ref[pair, at, :, :BLOCK_TOKENS] = left
            score_ref[pair, at, :, BLOCK_TOKENS:] = right

    def mix(pair, group, first):
        for at in range(GROUP):
            block = group * GROUP + at
            value_pair = jnp.concatenate(
                [keys_of(2 * pair, block, 1), keys_of(2 * pair + 1, block, 1)], axis=0
            )
            top = top_ref[at]
            top = jnp.concatenate([top, top], axis=1)
            weights = jnp.exp2((score_ref[pair, at] - top) * scale)
            total = weights[:, :BLOCK_TOKENS] + weights[:, BLOCK_TOKENS:]
            mixed = jnp.dot(
                weights.astype(jnp.bfloat16), value_pair, preferred_element_type=jnp.float32
            )
            if first:
                total_ref[at] = total
                mix_ref[at] = mixed
            else:
                total_ref[at] += total
                mix_ref[at] += mixed

    def group_step(group, carry):
        score(0, group, True)

        def score_step(pair, inner):
            score(pair, group, False)
            return inner

        lax.fori_loop(1, pairs, score_step, 0)
        for at in range(GROUP):
            top_ref[at] = jnp.broadcast_to(
                jnp.max(top_ref[at], axis=1, keepdims=True), (BLOCK_TOKENS, BLOCK_TOKENS)
            )
        mix(0, group, True)

        def mix_step(pair, inner):
            mix(pair, group, False)
            return inner

        lax.fori_loop(1, pairs, mix_step, 0)
        for at in range(GROUP):
            total = jnp.sum(total_ref[at], axis=1, keepdims=True)
            out_ref[group * GROUP + at] = (mix_ref[at] / total).astype(out_ref.dtype)
        return carry

    lax.fori_loop(0, SEG_BLOCKS // GROUP, group_step, 0)


def attention(index, bias, pairs, query, rows, columns):
    whole = (SEG_BLOCKS, BLOCK_TOKENS, HEAD_WIDTH)
    square = (GROUP, BLOCK_TOKENS, BLOCK_TOKENS)
    return pl.pallas_call(
        attention_kernel,
        out_shape=jax.ShapeDtypeStruct(whole, jnp.bfloat16),
        grid_spec=pltpu.PrefetchScalarGridSpec(
            num_scalar_prefetch=3,
            grid=(1,),
            in_specs=[pl.BlockSpec(whole, lambda i, *refs: (0, 0, 0))]
            + [pl.BlockSpec(memory_space=pl.ANY)] * (2 * len(PART_SIZES) + 1),
            out_specs=pl.BlockSpec(whole, lambda i, *refs: (0, 0, 0)),
            scratch_shapes=[
                pltpu.VMEM((POOL_BLOCKS, 2, BLOCK_TOKENS, HEAD_WIDTH), jnp.bfloat16),
                pltpu.VMEM((SLOTS // 2, GROUP, BLOCK_TOKENS, 2 * BLOCK_TOKENS), jnp.float32),
                pltpu.VMEM(square, jnp.float32),
                pltpu.VMEM(square, jnp.float32),
                pltpu.VMEM(square, jnp.float32),
                pltpu.SemaphoreType.DMA((2 * len(PART_SIZES) + 1,)),
            ],
        ),
        name="attention",
    )(index, bias, pairs, query, *rows, columns)


def slot_tables(columns, offsets, in_use, segment, x_index):
    slots = jnp.arange(SLOTS, dtype=jnp.int32)
    local = jnp.arange(SEG_BLOCKS, dtype=jnp.int32)
    blocks = segment * SEG_BLOCKS + local
    live_slash = jnp.arange(NS, dtype=jnp.int32) < in_use[1]
    slash_hit = slots[:, None] - 1 == jnp.arange(NS, dtype=jnp.int32)[None, :]
    offset = jnp.sum(jnp.where(slash_hit & live_slash[None, :], offsets[None, :], 0), axis=1)
    is_slash = (slots >= 1) & (slots <= in_use[1])
    column_slot = slots - 1 - in_use[1]
    is_column = (column_slot >= 0) & (column_slot < in_use[0])
    column_hit = column_slot[:, None] == jnp.arange(NV, dtype=jnp.int32)[None, :]
    column = jnp.sum(jnp.where(column_hit, columns[None, :], 0), axis=1)
    repeated = jnp.any(
        live_slash[None, None, :]
        & (blocks[None, :, None] - column[:, None, None] == offsets[None, None, :]),
        axis=2,
    )
    column_ok = is_column[:, None] & (column[:, None] < blocks[None, :]) & ~repeated
    slash_ok = is_slash[:, None] & (blocks[None, :] >= offset[:, None])
    source = local[None, :] - offset[:, None] + SEG_BLOCKS
    own = source // SEG_BLOCKS
    inner = source % SEG_BLOCKS
    turn = (x_index - inner // ROW_BLOCKS) % X_CHIPS
    near = own * SEG_BLOCKS + turn * ROW_BLOCKS + inner % ROW_BLOCKS
    far = jnp.clip(COLUMN_BASE + column_slot, COLUMN_BASE, POOL_BLOCKS - 1)
    index = jnp.where(is_column[:, None], far[:, None], near)
    active = (slots == 0)[:, None] | slash_ok | column_ok
    bias = jnp.where(active, 0.0, -jnp.inf).astype(jnp.float32)
    pairs = (in_use[0] + in_use[1] + 2) // 2
    return index.astype(jnp.int32), bias, pairs.astype(jnp.int32).reshape(1)


def shards(queries, key_row_matrix, values, verticals, slashes, counts):
    segment = lax.axis_index("seq")
    x_index = lax.axis_index("x")
    head = lax.axis_index("z") * X_CHIPS + x_index
    columns = lax.dynamic_index_in_dim(verticals, head, 0, keepdims=False)
    offsets = lax.dynamic_index_in_dim(slashes, head, 0, keepdims=False)
    in_use = lax.dynamic_index_in_dim(counts, head, 0, keepdims=False)

    tile = (BLOCK_TOKENS, KEY_VALUE_HEADS, HEAD_WIDTH)
    both = jnp.stack(
        [key_row_matrix.reshape(tile), values.reshape(tile)], axis=0
    ).transpose(2, 0, 1, 3)
    row = lax.all_to_all(both, "z", split_axis=0, concat_axis=0, tiled=True)
    after = shifted(row, "x", 1, X_CHIPS, True)
    before = shifted(row, "x", X_CHIPS - 1, X_CHIPS, True)
    earlier0 = shifted(row, "seq", 1, SEGMENTS, False)
    half = ROW_BLOCKS // 2
    across = [
        shifted(after[:half], "x", 1, X_CHIPS, True),
        shifted(before[half:], "x", X_CHIPS - 1, X_CHIPS, True),
    ]
    earlier1 = shifted(after, "seq", 1, SEGMENTS, False)
    earlier3 = shifted(before, "seq", 1, SEGMENTS, False)
    earlier2 = [shifted(part, "seq", 1, SEGMENTS, False) for part in across]
    rows = [row, after] + across + [before]
    earlier = [earlier0, earlier1] + earlier2 + [earlier3]

    inner = columns % SEG_BLOCKS
    turn = (x_index - inner // ROW_BLOCKS) % X_CHIPS
    place = jnp.where(
        columns // SEG_BLOCKS == segment, turn * ROW_BLOCKS + inner % ROW_BLOCKS, -1
    )
    mine = own_columns(place.astype(jnp.int32), rows)
    chunk = (SEGMENTS, NV * 2 * BLOCK_TOKENS // SEGMENTS, HEAD_WIDTH)
    pieces = lax.all_to_all(
        mine.reshape(chunk), "seq", split_axis=0, concat_axis=0, tiled=True
    )
    piece = pieces.astype(jnp.float32).sum(0).astype(jnp.bfloat16)
    wide = jnp.broadcast_to(piece[None], chunk)
    found = lax.all_to_all(wide, "seq", split_axis=0, concat_axis=0, tiled=True)
    found = found.reshape(NV, 2, BLOCK_TOKENS, HEAD_WIDTH)

    query = queries.reshape(BLOCK_TOKENS, Z_CHIPS, X_CHIPS, HEAD_WIDTH)
    query = query.transpose(2, 1, 0, 3).reshape(QUERY_HEADS, BLOCK_TOKENS, HEAD_WIDTH)
    query_here = lax.all_to_all(
        query, ("x", "z"), split_axis=0, concat_axis=0, tiled=True
    )

    index, bias, pairs = slot_tables(columns, offsets, in_use, segment, x_index)
    context = attention(index, bias, pairs, query_here, earlier + rows, found)
    back = lax.all_to_all(context, ("x", "z"), split_axis=0, concat_axis=0, tiled=True)
    back = back.reshape(X_CHIPS, Z_CHIPS, BLOCK_TOKENS, HEAD_WIDTH).transpose(2, 1, 0, 3)
    return back.reshape(1, BLOCK_TOKENS, QUERY_HEADS * HEAD_WIDTH)


def solution(mesh):
    fine = Mesh(mesh.devices.reshape(X_CHIPS, Z_CHIPS, SEGMENTS), ("x", "z", "seq"))
    spread = P("seq", ("x", "z"), None)
    return jax.shard_map(
        shards,
        mesh=fine,
        in_specs=(spread, spread, spread, P(), P(), P()),
        out_specs=spread,
        check_vma=False,
    )
```

profile of v0, /device:TPU:16, one launch (start us, length us, event | category | flops | bytes accessed | tf_op | source)
XLA Modules:
  0.0 217.0 jit_solution(8201662427895164946)
XLA Ops:
  0.0 1.1 copy.17
  1.2 0.2 copy.19
  1.3 0.8 copy-done.14
  2.3 0.2 copy.18
  2.5 27.6 %all_to_all.25.refs_0_.rest_5_ = bf16[8,2,128,128]{3,2,1,0:T(8,128)(2,1)S(1)} all-to-all(bf16[8,2,128,128]{3,2,1,0:T(8,128)(2,1)S(1)} %maximum_bitcast_fusion), channel_id=1, replica_groups=mesh['x'=4,'z'=8,'seq'=16] {'z'}, dimensions={0} | all-to-all | bytes 1048576 | tf_op jit(solution)/shard_map/all_to_all | solution.py:238
  30.1 3.4 %collective-permute-start.1 = (bf16[8,2,128,128]{3,2,1,0:T(8,128)(2,1)S(1)}, bf16[8,2,128,128]{3,2,1,0:T(8,128)(2,1)S(1)}, u32[]{:S(2)}, u32[]{:S(2)}) collective-permute-start(bf16[8,2,128,128]{3,2,1,0:T(8,128)(2,1)S(1)} %all_to_all.25.refs_0_.rest_5_), channel_id=1, source_target_pairs={{0,128},{128,256},{256,384},{384,0},{1,129},{129,257},{257,385},{3... | collective-permute-start | bytes 1572872 | tf_op jit(solution)/shard_map/ppermute | solution.py:31
  33.5 3.7 %collective-permute-start.5 = (bf16[8,2,128,128]{3,2,1,0:T(8,128)(2,1)S(1)}, bf16[8,2,128,128]{3,2,1,0:T(8,128)(2,1)S(1)}, u32[]{:S(2)}, u32[]{:S(2)}) collective-permute-start(bf16[8,2,128,128]{3,2,1,0:T(8,128)(2,1)S(1)} %all_to_all.25.refs_0_.rest_5_), channel_id=1, source_target_pairs={{0,384},{128,0},{256,128},{384,256},{1,385},{129,1},{257,129},{385... | collective-permute-start | bytes 1572872 | tf_op jit(solution)/shard_map/ppermute | solution.py:31
  37.2 8.0 %collective-permute-done.1.refs_1_.rest_6_ = bf16[8,2,128,128]{3,2,1,0:T(8,128)(2,1)S(1)} collective-permute-done((bf16[8,2,128,128]{3,2,1,0:T(8,128)(2,1)S(1)}, bf16[8,2,128,128]{3,2,1,0:T(8,128)(2,1)S(1)}, u32[]{:S(2)}, u32[]{:S(2)}) %collective-permute-start.1) | collective-permute-done | bytes 524320 | tf_op jit(solution)/shard_map/ppermute | solution.py:31
  45.3 2.2 %collective-permute-start.3 = (bf16[4,2,128,128]{3,2,1,0:T(8,128)(2,1)S(1)}, bf16[4,2,128,128]{3,2,1,0:T(8,128)(2,1)S(1)}, u32[]{:S(2)}, u32[]{:S(2)}) collective-permute-start(bf16[4,2,128,128]{3,2,1,0:T(8,128)(2,1)S(1)} %slice.22), channel_id=1, source_target_pairs={{0,128},{128,256},{256,384},{384,0},{1,129},{129,257},{257,385},{3... | collective-permute-start | bytes 786440 | tf_op jit(solution)/shard_map/ppermute | solution.py:31
  47.5 4.9 %collective-permute-start.6 = (bf16[4,2,128,128]{3,2,1,0:T(8,128)(2,1)S(1)}, bf16[4,2,128,128]{3,2,1,0:T(8,128)(2,1)S(1)}, u32[]{:S(2)}, u32[]{:S(2)}) collective-permute-start(bf16[4,2,128,128]{3,2,1,0:T(8,128)(2,1)S(1)} %slice.23), channel_id=1, source_target_pairs={{0,384},{128,0},{256,128},{384,256},{1,385},{129,1},{257,129},{385... | collective-permute-start | bytes 786440 | tf_op jit(solution)/shard_map/ppermute | solution.py:31
  52.4 0.2 dynamic-slice_reduce_fusion
  52.6 0.5 compare_select_fusion.2.place_ref
  53.1 1.6 collective-permute-done.3.refs_2_.rest_7_
  54.7 1.5 collective-permute-done.6.refs_3_.rest_8_
  56.3 0.7 copy-done.12
  57.0 3.2 %own_columns.1 = bf16[6,2,128,128]{3,2,1,0:T(8,128)(2,1)} custom-call(s32[6]{0:T(128)} %compare_select_fusion.2.place_ref, bf16[8,2,128,128]{3,2,1,0:T(8,128)(2,1)} %copy-done.1, bf16[8,2,128,128]{3,2,1,0:T(8,128)(2,1)} %copy-done.4, bf16[4,2,128,128]{3,2,1,0:T(8,128)(2,1)} %copy-done.10, bf16[4,2,128,128]{3,2,1,0:T(8,128)(2,1)} %copy-done.12, ...), custom_call_target="tpu_custom_call" | custom-call | tf_op jit(solution)/shard_map/own_columns/pallas_call | solution.py:56
  60.2 5.9 %all-to-all-start.2 = ((bf16[16,96,128]{2,1,0:T(8,128)(2,1)}), bf16[16,96,128]{2,1,0:T(8,128)(2,1)S(1)}, u32[]{:S(2)}, u32[]{:S(2)}) async-start(bf16[16,96,128]{2,1,0:T(8,128)(2,1)} %bitcast.16), calls=%async_computation.2 | async-start | bytes 786432 | tf_op jit(solution)/shard_map/all_to_all | solution.py:260
  66.1 0.8 reshape.108
  66.9 1.4 copy.15
  68.3 10.1 %all-to-all-done.2 = bf16[16,96,128]{2,1,0:T(8,128)(2,1)S(1)} async-done(((bf16[16,96,128]{2,1,0:T(8,128)(2,1)}), bf16[16,96,128]{2,1,0:T(8,128)(2,1)S(1)}, u32[]{:S(2)}, u32[]{:S(2)}) %all-to-all-start.2) | async-done | bytes 393248 | tf_op jit(solution)/shard_map/all_to_all | solution.py:260
  78.4 7.3 %all-to-all-start = ((bf16[32,128,128]{2,1,0:T(8,128)(2,1)}), bf16[32,128,128]{2,1,0:T(8,128)(2,1)S(1)}, u32[]{:S(2)}, u32[]{:S(2)}) async-start(bf16[32,128,128]{2,1,0:T(8,128)(2,1)} %bitcast.4), calls=%async_computation | async-start | bytes 2097152 | tf_op jit(solution)/shard_map/all_to_all | solution.py:270
  85.8 0.2 dynamic-slice_reduce_fusion.1
  86.0 0.7 copy-done.27
  86.7 0.6 fusion.15
  87.3 0.6 iota_compare_fusion.3
  88.0 0.6 broadcast_subtract_fusion.1
  88.6 1.8 compare_and_fusion.1
  90.6 0.7 select_reduce_fusion.1
  91.4 23.2 %all-to-all-done.query_ref = bf16[32,128,128]{2,1,0:T(8,128)(2,1)S(1)} async-done(((bf16[32,128,128]{2,1,0:T(8,128)(2,1)}), bf16[32,128,128]{2,1,0:T(8,128)(2,1)S(1)}, u32[]{:S(2)}, u32[]{:S(2)}) %all-to-all-start) | async-done | bytes 1048608 | tf_op jit(solution)/shard_map/all_to_all | solution.py:270
  114.6 0.9 broadcast_in_dim.92
  115.5 5.1 %all-to-all-start.3 = ((bf16[16,96,128]{2,1,0:T(8,128)(2,1)}), bf16[16,96,128]{2,1,0:T(8,128)(2,1)S(1)}, u32[]{:S(2)}, u32[]{:S(2)}) async-start(bf16[16,96,128]{2,1,0:T(8,128)(2,1)} %broadcast_in_dim.92), calls=%async_computation.3 | async-start | bytes 786432 | tf_op jit(solution)/shard_map/all_to_all | solution.py:265
  120.6 0.6 add_clamp_fusion
  121.4 2.0 collective-permute-start
  123.5 3.4 %collective-permute-start.2 = (bf16[8,2,128,128]{3,2,1,0:T(8,128)(2,1)S(1)}, bf16[8,2,128,128]{3,2,1,0:T(8,128)(2,1)}, u32[]{:S(2)}, u32[]{:S(2)}) collective-permute-start(bf16[8,2,128,128]{3,2,1,0:T(8,128)(2,1)S(1)} %copy-done.5), channel_id=1, source_target_pairs={{0,1},{1,2},{2,3},{3,4},{4,5},{5,6},{6,7},{7,8},{8,9},{9,10},{10,1... | collective-permute-start | bytes 1572872 | tf_op jit(solution)/shard_map/ppermute | solution.py:31
  126.8 2.0 collective-permute-start.8
  128.9 0.7 fusion.3.index_ref
  129.6 4.6 %collective-permute-start.4 = (bf16[4,2,128,128]{3,2,1,0:T(8,128)(2,1)S(1)}, bf16[4,2,128,128]{3,2,1,0:T(8,128)(2,1)}, u32[]{:S(2)}, u32[]{:S(2)}) collective-permute-start(bf16[4,2,128,128]{3,2,1,0:T(8,128)(2,1)S(1)} %copy-done.11), channel_id=1, source_target_pairs={{0,1},{1,2},{2,3},{3,4},{4,5},{5,6},{6,7},{7,8},{8,9},{9,10},{10,1... | collective-permute-start | bytes 786440 | tf_op jit(solution)/shard_map/ppermute | solution.py:31
  134.2 2.0 collective-permute-start.7
  136.2 1.1 compare_and_fusion
  138.7 0.6 copy-done.23
  139.3 1.2 or_select_fusion.bias_ref
  140.6 9.8 %collective-permute-done.4.rest_2_ = bf16[4,2,128,128]{3,2,1,0:T(8,128)(2,1)} collective-permute-done((bf16[4,2,128,128]{3,2,1,0:T(8,128)(2,1)S(1)}, bf16[4,2,128,128]{3,2,1,0:T(8,128)(2,1)}, u32[]{:S(2)}, u32[]{:S(2)}) %collective-permute-start.4) | collective-permute-done | bytes 262176 | tf_op jit(solution)/shard_map/ppermute | solution.py:31
  150.4 2.8 %collective-permute-done.7.rest_3_ = bf16[4,2,128,128]{3,2,1,0:T(8,128)(2,1)} collective-permute-done((bf16[4,2,128,128]{3,2,1,0:T(8,128)(2,1)S(1)}, bf16[4,2,128,128]{3,2,1,0:T(8,128)(2,1)}, u32[]{:S(2)}, u32[]{:S(2)}) %collective-permute-start.7) | collective-permute-done | bytes 262176 | tf_op jit(solution)/shard_map/ppermute | solution.py:31
  153.2 0.7 copy-done.8
  153.9 11.0 %attention.1 = bf16[32,128,128]{2,1,0:T(8,128)(2,1)} custom-call(s32[10,32]{1,0:T(8,128)} %fusion.3.index_ref, f32[10,32]{1,0:T(8,128)} %or_select_fusion.bias_ref, s32[1]{0:T(128)} %bitcast.2.pairs_ref, bf16[32,128,128]{2,1,0:T(8,128)(2,1)} %copy-done.3, bf16[8,2,128,128]{3,2,1,0:T(8,128)(2,1)} %collective-permute-done.rest_0_, ...), custom_call_target="tpu_custom_call" | custom-call | tf_op jit(solution)/shard_map/attention/pallas_call | solution.py:172
  165.0 49.6 %all_to_all.26 = bf16[32,128,128]{2,1,0:T(8,128)(2,1)S(1)} all-to-all(bf16[32,128,128]{2,1,0:T(8,128)(2,1)} %attention.1), channel_id=1, replica_groups=mesh['x'=4,'z'=8,'seq'=16] {'x','z'}, dimensions={0} | all-to-all | bytes 2097152 | tf_op jit(solution)/shard_map/all_to_all | solution.py:276
  214.6 0.8 copy.20
  215.4 1.6 reshape.113
  (67 shorter events, 0.9 us)
Async XLA Ops:
  0.0 52.4 %copy-start = (s32[32,6]{0,1:T(8,128)S(1)}, s32[32,6]{0,1:T(8,128)}, u32[]{:S(2)}) copy-start(s32[32,6]{0,1:T(8,128)} %param.9) | copy-start | bytes 2308
  1.1 1.0 copy-start.14
  30.1 17.4 %copy-start.1 = (bf16[8,2,128,128]{3,2,1,0:T(8,128)(2,1)}, bf16[8,2,128,128]{3,2,1,0:T(8,128)(2,1)S(1)}, u32[]{:S(2)}) copy-start(bf16[8,2,128,128]{3,2,1,0:T(8,128)(2,1)S(1)} %all_to_all.25.refs_0_.rest_5_) | copy-start | bytes 1572868
  30.1 15.1 %collective-permute-start.1 = (bf16[8,2,128,128]{3,2,1,0:T(8,128)(2,1)S(1)}, bf16[8,2,128,128]{3,2,1,0:T(8,128)(2,1)S(1)}, u32[]{:S(2)}, u32[]{:S(2)}) collective-permute-start(bf16[8,2,128,128]{3,2,1,0:T(8,128)(2,1)S(1)} %all_to_all.25.refs_0_.rest_5_), channel_id=1, source_target_pairs={{0,128},{128,256},{256,384},{384,0},{1,129},{129,257},{257,385},{3... | collective-permute-start | bytes 1572872 | tf_op jit(solution)/shard_map/ppermute | solution.py:31
  33.5 13.9 %collective-permute-start.5 = (bf16[8,2,128,128]{3,2,1,0:T(8,128)(2,1)S(1)}, bf16[8,2,128,128]{3,2,1,0:T(8,128)(2,1)S(1)}, u32[]{:S(2)}, u32[]{:S(2)}) collective-permute-start(bf16[8,2,128,128]{3,2,1,0:T(8,128)(2,1)S(1)} %all_to_all.25.refs_0_.rest_5_), channel_id=1, source_target_pairs={{0,384},{128,0},{256,128},{384,256},{1,385},{129,1},{257,129},{385... | collective-permute-start | bytes 1572872 | tf_op jit(solution)/shard_map/ppermute | solution.py:31
  45.2 2.3 %copy-start.4 = (bf16[8,2,128,128]{3,2,1,0:T(8,128)(2,1)}, bf16[8,2,128,128]{3,2,1,0:T(8,128)(2,1)S(1)}, u32[]{:S(2)}) copy-start(bf16[8,2,128,128]{3,2,1,0:T(8,128)(2,1)S(1)} %collective-permute-done.1.refs_1_.rest_6_) | copy-start | bytes 1572868
  45.3 9.5 %collective-permute-start.3 = (bf16[4,2,128,128]{3,2,1,0:T(8,128)(2,1)S(1)}, bf16[4,2,128,128]{3,2,1,0:T(8,128)(2,1)S(1)}, u32[]{:S(2)}, u32[]{:S(2)}) collective-permute-start(bf16[4,2,128,128]{3,2,1,0:T(8,128)(2,1)S(1)} %slice.22), channel_id=1, source_target_pairs={{0,128},{128,256},{256,384},{384,0},{1,129},{129,257},{257,385},{3... | collective-permute-start | bytes 786440 | tf_op jit(solution)/shard_map/ppermute | solution.py:31
  47.5 8.8 %copy-start.6 = (bf16[8,2,128,128]{3,2,1,0:T(8,128)(2,1)}, bf16[8,2,128,128]{3,2,1,0:T(8,128)(2,1)S(1)}, u32[]{:S(2)}) copy-start(bf16[8,2,128,128]{3,2,1,0:T(8,128)(2,1)S(1)} %collective-permute-done.5.refs_4_.rest_9_) | copy-start | bytes 1572868
  47.5 8.7 %collective-permute-start.6 = (bf16[4,2,128,128]{3,2,1,0:T(8,128)(2,1)S(1)}, bf16[4,2,128,128]{3,2,1,0:T(8,128)(2,1)S(1)}, u32[]{:S(2)}, u32[]{:S(2)}) collective-permute-start(bf16[4,2,128,128]{3,2,1,0:T(8,128)(2,1)S(1)} %slice.23), channel_id=1, source_target_pairs={{0,384},{128,0},{256,128},{384,256},{1,385},{129,1},{257,129},{385... | collective-permute-start | bytes 786440 | tf_op jit(solution)/shard_map/ppermute | solution.py:31
  53.1 13.0 %copy-start.9 = (bf16[1,128,4096]{2,1,0:T(8,128)(2,1)S(1)}, bf16[1,128,4096]{2,1,0:T(8,128)(2,1)}, u32[]{:S(2)}) copy-start(bf16[1,128,4096]{2,1,0:T(8,128)(2,1)} %param.6) | copy-start | bytes 3145732
  54.7 1.5 copy-start.10
  56.3 0.7 copy-start.12
  60.2 18.2 %all-to-all-start.2 = ((bf16[16,96,128]{2,1,0:T(8,128)(2,1)}), bf16[16,96,128]{2,1,0:T(8,128)(2,1)S(1)}, u32[]{:S(2)}, u32[]{:S(2)}) async-start(bf16[16,96,128]{2,1,0:T(8,128)(2,1)} %bitcast.16), calls=%async_computation.2 | async-start | bytes 786432 | tf_op jit(solution)/shard_map/all_to_all | solution.py:260
  78.4 7.4 %copy-start.19 = (s32[32,3]{0,1:T(4,128)S(1)}, s32[32,3]{0,1:T(4,128)}, u32[]{:S(2)}) copy-start(s32[32,3]{0,1:T(4,128)} %param.10) | copy-start | bytes 1156
  78.4 51.2 %copy-start.11 = (bf16[4,2,128,128]{3,2,1,0:T(8,128)(2,1)S(1)}, bf16[4,2,128,128]{3,2,1,0:T(8,128)(2,1)}, u32[]{:S(2)}) copy-start(bf16[4,2,128,128]{3,2,1,0:T(8,128)(2,1)} %copy-done.10) | copy-start | bytes 786436
  78.4 55.8 %copy-start.13 = (bf16[4,2,128,128]{3,2,1,0:T(8,128)(2,1)S(1)}, bf16[4,2,128,128]{3,2,1,0:T(8,128)(2,1)}, u32[]{:S(2)}) copy-start(bf16[4,2,128,128]{3,2,1,0:T(8,128)(2,1)} %copy-done.12) | copy-start | bytes 786436
  78.4 36.2 %all-to-all-start = ((bf16[32,128,128]{2,1,0:T(8,128)(2,1)}), bf16[32,128,128]{2,1,0:T(8,128)(2,1)S(1)}, u32[]{:S(2)}, u32[]{:S(2)}) async-start(bf16[32,128,128]{2,1,0:T(8,128)(2,1)} %bitcast.4), calls=%async_computation | async-start | bytes 2097152 | tf_op jit(solution)/shard_map/all_to_all | solution.py:270
  86.0 4.6 %copy-start.15 = (s32[3]{0:T(128)}, s32[3]{0:T(128)S(1)}, u32[]{:S(2)}) copy-start(s32[3]{0:T(128)S(1)} %dynamic-slice_reduce_fusion.1) | copy-start | bytes 40
  86.0 0.7 copy-start.27
  87.9 2.6 %copy-start.20 = (pred[3]{0:T(512)(128)(4,1)}, pred[3]{0:T(512)(128)(4,1)S(1)}, u32[]{:S(2)}) copy-start(pred[3]{0:T(512)(128)(4,1)S(1)} %iota_compare_fusion.3) | copy-start | bytes 13
  88.6 2.6 %copy-start.22 = (s32[32]{0:T(128)}, s32[32]{0:T(128)S(1)}, u32[]{:S(2)}) copy-start(s32[32]{0:T(128)S(1)} %iota_add_fusion) | copy-start | bytes 388
  90.6 0.7 copy-start.24
  91.3 35.5 %copy-start.7 = (bf16[8,2,128,128]{3,2,1,0:T(8,128)(2,1)S(1)}, bf16[8,2,128,128]{3,2,1,0:T(8,128)(2,1)}, u32[]{:S(2)}) copy-start(bf16[8,2,128,128]{3,2,1,0:T(8,128)(2,1)} %copy-done.6) | copy-start | bytes 1572868
  91.4 30.0 %copy-start.2 = (bf16[8,2,128,128]{3,2,1,0:T(8,128)(2,1)S(1)}, bf16[8,2,128,128]{3,2,1,0:T(8,128)(2,1)}, u32[]{:S(2)}) copy-start(bf16[8,2,128,128]{3,2,1,0:T(8,128)(2,1)} %copy-done.1) | copy-start | bytes 1572868
  91.4 32.1 %copy-start.5 = (bf16[8,2,128,128]{3,2,1,0:T(8,128)(2,1)S(1)}, bf16[8,2,128,128]{3,2,1,0:T(8,128)(2,1)}, u32[]{:S(2)}) copy-start(bf16[8,2,128,128]{3,2,1,0:T(8,128)(2,1)} %copy-done.4) | copy-start | bytes 1572868
  114.6 38.6 %copy-start.3 = (bf16[32,128,128]{2,1,0:T(8,128)(2,1)}, bf16[32,128,128]{2,1,0:T(8,128)(2,1)S(1)}, u32[]{:S(2)}) copy-start(bf16[32,128,128]{2,1,0:T(8,128)(2,1)S(1)} %all-to-all-done.query_ref) | copy-start | bytes 3145732
  115.5 37.7 %all-to-all-start.3 = ((bf16[16,96,128]{2,1,0:T(8,128)(2,1)}), bf16[16,96,128]{2,1,0:T(8,128)(2,1)S(1)}, u32[]{:S(2)}, u32[]{:S(2)}) async-start(bf16[16,96,128]{2,1,0:T(8,128)(2,1)} %broadcast_in_dim.92), calls=%async_computation.3 | async-start | bytes 786432 | tf_op jit(solution)/shard_map/all_to_all | solution.py:265
  120.6 0.7 copy-start.16
  120.6 0.7 copy-start.21
  121.4 7.5 %copy-start.17 = (pred[10]{0:T(512)(128)(4,1)S(1)}, pred[10]{0:T(512)(128)(4,1)}, u32[]{:S(2)}) copy-start(pred[10]{0:T(512)(128)(4,1)} %get-tuple-element.7) | copy-start | bytes 34
  121.4 7.5 %copy-start.18 = (s32[10]{0:T(128)S(1)}, s32[10]{0:T(128)}, u32[]{:S(2)}) copy-start(s32[10]{0:T(128)} %select_reduce_fusion.1) | copy-start | bytes 124
  121.4 19.2 %collective-permute-start = (bf16[8,2,128,128]{3,2,1,0:T(8,128)(2,1)S(1)}, bf16[8,2,128,128]{3,2,1,0:T(8,128)(2,1)}, u32[]{:S(2)}, u32[]{:S(2)}) collective-permute-start(bf16[8,2,128,128]{3,2,1,0:T(8,128)(2,1)S(1)} %copy-done.2), channel_id=1, source_target_pairs={{0,1},{1,2},{2,3},{3,4},{4,5},{5,6},{6,7},{7,8},{8,9},{9,10},{10,1... | collective-permute-start | bytes 1572872 | tf_op jit(solution)/shard_map/ppermute | solution.py:31
  123.5 29.7 %collective-permute-start.2 = (bf16[8,2,128,128]{3,2,1,0:T(8,128)(2,1)S(1)}, bf16[8,2,128,128]{3,2,1,0:T(8,128)(2,1)}, u32[]{:S(2)}, u32[]{:S(2)}) collective-permute-start(bf16[8,2,128,128]{3,2,1,0:T(8,128)(2,1)S(1)} %copy-done.5), channel_id=1, source_target_pairs={{0,1},{1,2},{2,3},{3,4},{4,5},{5,6},{6,7},{7,8},{8,9},{9,10},{10,1... | collective-permute-start | bytes 1572872 | tf_op jit(solution)/shard_map/ppermute | solution.py:31
  126.8 26.3 %collective-permute-start.8 = (bf16[8,2,128,128]{3,2,1,0:T(8,128)(2,1)S(1)}, bf16[8,2,128,128]{3,2,1,0:T(8,128)(2,1)}, u32[]{:S(2)}, u32[]{:S(2)}) collective-permute-start(bf16[8,2,128,128]{3,2,1,0:T(8,128)(2,1)S(1)} %copy-done.7), channel_id=1, source_target_pairs={{0,1},{1,2},{2,3},{3,4},{4,5},{5,6},{6,7},{7,8},{8,9},{9,10},{10,1... | collective-permute-start | bytes 1572872 | tf_op jit(solution)/shard_map/ppermute | solution.py:31
  129.6 20.8 %collective-permute-start.4 = (bf16[4,2,128,128]{3,2,1,0:T(8,128)(2,1)S(1)}, bf16[4,2,128,128]{3,2,1,0:T(8,128)(2,1)}, u32[]{:S(2)}, u32[]{:S(2)}) collective-permute-start(bf16[4,2,128,128]{3,2,1,0:T(8,128)(2,1)S(1)} %copy-done.11), channel_id=1, source_target_pairs={{0,1},{1,2},{2,3},{3,4},{4,5},{5,6},{6,7},{7,8},{8,9},{9,10},{10,1... | collective-permute-start | bytes 786440 | tf_op jit(solution)/shard_map/ppermute | solution.py:31
  134.2 19.0 %collective-permute-start.7 = (bf16[4,2,128,128]{3,2,1,0:T(8,128)(2,1)S(1)}, bf16[4,2,128,128]{3,2,1,0:T(8,128)(2,1)}, u32[]{:S(2)}, u32[]{:S(2)}) collective-permute-start(bf16[4,2,128,128]{3,2,1,0:T(8,128)(2,1)S(1)} %copy-done.13), channel_id=1, source_target_pairs={{0,1},{1,2},{2,3},{3,4},{4,5},{5,6},{6,7},{7,8},{8,9},{9,10},{10,1... | collective-permute-start | bytes 786440 | tf_op jit(solution)/shard_map/ppermute | solution.py:31
  138.6 0.6 copy-start.23
  138.6 0.6 copy-start.25
  138.6 0.7 copy-start.26
  153.2 0.7 copy-start.8
where the time goes:
time: 218 us; the launch traced here: 217 us
  blocking collectives  77.2 us (35%)
  waiting for transfers between devices  57.1 us (26%)
  starting transfers between devices  46.5 us (21%)
  Pallas kernels  14.3 us (7%)
  local copies, waits for them, and re-layouts  11.8 us (5%)
  other arithmetic  8.4 us (4%)
    all_to_all x1, blocking collectives, shards(): lax.all_to_all(context, ('x', 'z'), split_axis=0, concat_axis=0, tiled=True)  49.6 us
    ppermute x9, starting transfers between devices, shifted(): return lax.ppermute(value, axis, pairs)  28.1 us
    all_to_all x1, blocking collectives, shards(): row = lax.all_to_all(both, 'z', split_axis=0, concat_axis=0, tiled=True)  27.6 us
    ppermute x9, waiting for transfers between devices, shifted(): return lax.ppermute(value, axis, pairs)  23.8 us
    all_to_all x1, waiting for transfers between devices, shards(): lax.all_to_all(query, ('x', 'z'), split_axis=0, concat_axis=0, tiled=True)  23.2 us
    pallas_call x1, Pallas kernels, attention(): pl.pallas_call(attention_kernel, out_shape=jax.ShapeDtypeStruct(whole, jn...  11 us
    all_to_all x1, waiting for transfers between devices, shards(): lax.all_to_all(mine.reshape(chunk), 'seq', split_axis=0, concat_axis=0, t...  10.1 us
    all_to_all x1, starting transfers between devices, shards(): lax.all_to_all(query, ('x', 'z'), split_axis=0, concat_axis=0, tiled=True)  7.35 us
  transfers between devices with their start and end apart: 12, of which 7 were waited for; matrix products, arithmetic and copies ran while one was open for 5% of the time, Pallas kernels for 0%

commit v1 on v0

v1 whole, which is shorter than its diff:
```python
import math

import jax
import jax.numpy as jnp
from jax import lax
from jax.experimental import pallas as pl
from jax.experimental.pallas import tpu as pltpu
from jax.sharding import Mesh
from jax.sharding import PartitionSpec as P


QUERY_HEADS = 32
KEY_VALUE_HEADS = 8
HEAD_WIDTH = 128
BLOCK_TOKENS = 128
X_CHIPS = 4
Z_CHIPS = 8
SEGMENTS = 16
NV = 6
NS = 3
SEG_BLOCKS = 32
GROUP = X_CHIPS
SCALE = math.log2(math.e) / math.sqrt(HEAD_WIDTH)
SQUARE = (BLOCK_TOKENS, HEAD_WIDTH)
PART_STARTS = (0, 8, 16, 20, 24)
PART_SIZES = (8, 8, 4, 4, 8)
PARTS = len(PART_SIZES)


def shifted(value, axis, distance, size, wrap):
    pairs = [(i, (i + distance) % size) for i in range(size) if wrap or i + distance < size]
    return lax.ppermute(value, axis, pairs)


def scalars(count):
    return [pl.BlockSpec(memory_space=pltpu.SMEM)] * count


def pack_kernel(key_ref, value_ref, out_ref):
    for head in range(KEY_VALUE_HEADS):
        lanes = slice(head * HEAD_WIDTH, (head + 1) * HEAD_WIDTH)
        out_ref[head, 0] = key_ref[:, lanes]
        out_ref[head, 1] = value_ref[:, lanes]


def packed(keys, values):
    return pl.pallas_call(
        pack_kernel,
        out_shape=jax.ShapeDtypeStruct((KEY_VALUE_HEADS, 2) + SQUARE, jnp.bfloat16),
        name="packed",
    )(keys, values)


def deal_kernel(place_ref, query_ref, *out_refs):
    x_index = place_ref[1]
    for turn, out_ref in enumerate(out_refs):
        column = (x_index + turn) & (X_CHIPS - 1)
        for row in range(Z_CHIPS):
            start = pl.multiple_of((row * X_CHIPS + column) * HEAD_WIDTH, HEAD_WIDTH)
            out_ref[row] = query_ref[:, pl.ds(start, HEAD_WIDTH)]


def dealt(place, query):
    whole = pl.BlockSpec(memory_space=pltpu.VMEM)
    return pl.pallas_call(
        deal_kernel,
        out_shape=[jax.ShapeDtypeStruct((Z_CHIPS,) + SQUARE, jnp.bfloat16)] * X_CHIPS,
        in_specs=scalars(1) + [whole],
        out_specs=[whole] * X_CHIPS,
        name="dealt",
    )(place, query)


def pool_index(source, x_index):
    own = source >> 5
    inner = source & (SEG_BLOCKS - 1)
    turn = (x_index - (inner >> 3)) & (X_CHIPS - 1)
    return own * SEG_BLOCKS + turn * Z_CHIPS + (inner & (Z_CHIPS - 1))


def column_kernel(place_ref, vertical_ref, *refs):
    parts = refs[:PARTS]
    out_ref, sems = refs[PARTS:]
    segment, x_index, head = place_ref[0], place_ref[1], place_ref[2]
    out_ref[...] = jnp.zeros_like(out_ref)
    for slot in range(NV):
        column = vertical_ref[head, slot]
        at = pool_index(column & (SEG_BLOCKS - 1), x_index)
        mine = (column >> 5) == segment
        for part, low, size in zip(parts, PART_STARTS, PART_SIZES):

            @pl.when(mine & (at >= low) & (at < low + size))
            def _():
                copy = pltpu.make_async_copy(
                    part.at[at - low], out_ref.at[slot], sems.at[slot]
                )
                copy.start()
                copy.wait()


def own_columns(place, verticals, parts):
    return pl.pallas_call(
        column_kernel,
        out_shape=jax.ShapeDtypeStruct((NV, 2) + SQUARE, jnp.bfloat16),
        in_specs=scalars(2) + [pl.BlockSpec(memory_space=pl.ANY)] * PARTS,
        out_specs=pl.BlockSpec(memory_space=pltpu.VMEM),
        scratch_shapes=[pltpu.SemaphoreType.DMA((NV,))],
        name="own_columns",
    )(place, verticals, *parts)


def two_blocks(pool, left, right, part):
    return jnp.concatenate([pool[left, part], pool[right, part]], axis=0)


def scores_of(query, keys):
    return lax.dot_general(
        query, keys, (((1,), (1,)), ((), ())), preferred_element_type=jnp.float32
    )


def weigh(score_ref, top_ref, pair, at):
    top = top_ref[at]
    top = jnp.concatenate([top, top], axis=1)
    weights = jnp.exp2((score_ref[pair, at] - top) * SCALE)
    total = weights[:, :BLOCK_TOKENS] + weights[:, BLOCK_TOKENS:]
    return weights.astype(jnp.bfloat16), total


def bias_of(active):
    return jnp.where(active, 0.0, -jnp.inf).astype(jnp.float32)


def wide_top(top):
    return jnp.broadcast_to(jnp.max(top, axis=1, keepdims=True), SQUARE)


def near_kernel(place_ref, slash_ref, count_ref, query_ref, *refs):
    parts = refs[: 2 * PARTS]
    mix_ref, stat_ref, pool, score_ref, top_ref, total_ref, sems = refs[2 * PARTS :]
    step = pl.program_id(0)
    segment, x_index, head = place_ref[0], place_ref[1], place_ref[2]
    used = count_ref[head, 1]
    pairs = (used + 2) >> 1

    @pl.when(step == 0)
    def _():
        starts = PART_STARTS + tuple(SEG_BLOCKS + start for start in PART_STARTS)
        copies = [
            pltpu.make_async_copy(part, pool.at[pl.ds(start, size)], sems.at[at])
            for at, (part, start, size) in enumerate(zip(parts, starts, PART_SIZES * 2))
        ]
        for copy in copies:
            copy.start()
        for copy in copies:
            copy.wait()

    blocks = [((x_index - at) & (X_CHIPS - 1)) * Z_CHIPS + step for at in range(GROUP)]
    row_ids = lax.broadcasted_iota(jnp.int32, SQUARE, 0)
    col_ids = lax.broadcasted_iota(jnp.int32, SQUARE, 1)

    def offset_of(slot):
        live = slot <= used
        return jnp.where(live, slash_ref[head, jnp.clip(slot - 1, 0, NS - 1)], 0), live

    def place_of(offset, block):
        return pool_index(block - offset + SEG_BLOCKS, x_index)

    def score(pair, first):
        offsets = [(0, True) if first else offset_of(2 * pair), offset_of(2 * pair + 1)]
        for at, block in enumerate(blocks):
            spots = [place_of(offset, block) for offset, _ in offsets]
            found = scores_of(query_ref[0, at], two_blocks(pool, *spots, 0))
            reach = segment * SEG_BLOCKS + block
            right = found[:, BLOCK_TOKENS:] + bias_of(
                offsets[1][1] & (reach >= offsets[1][0])
            )
            left = found[:, :BLOCK_TOKENS]
            if first:
                left = jnp.where(row_ids >= col_ids, left, -jnp.inf)
                top_ref[at] = jnp.maximum(left, right)
            else:
                left = left + bias_of(offsets[0][1] & (reach >= offsets[0][0]))
                top_ref[at] = jnp.maximum(top_ref[at], jnp.maximum(left, right))
            score_ref[pair, at, :, :BLOCK_TOKENS] = left
            score_ref[pair, at, :, BLOCK_TOKENS:] = right

    def mix(pair, first):
        offsets = [0 if first else offset_of(2 * pair)[0], offset_of(2 * pair + 1)[0]]
        for at, block in enumerate(blocks):
            spots = [place_of(offset, block) for offset in offsets]
            weights, total = weigh(score_ref, top_ref, pair, at)
            mixed = jnp.dot(
                weights, two_blocks(pool, *spots, 1), preferred_element_type=jnp.float32
            )
            if first:
                total_ref[at] = total
                mix_ref[0, at] = mixed
            else:
                total_ref[at] += total
                mix_ref[0, at] += mixed

    score(0, True)

    @pl.when(pairs > 1)
    def _():
        score(1, False)

    for at in range(GROUP):
        top_ref[at] = wide_top(top_ref[at])
    mix(0, True)

    @pl.when(pairs > 1)
    def _():
        mix(1, False)

    for at in range(GROUP):
        total = jnp.sum(total_ref[at], axis=1, keepdims=True)
        stat_ref[0, at] = jnp.where(
            col_ids < BLOCK_TOKENS // 2, top_ref[at], jnp.broadcast_to(total, SQUARE)
        )


def near_part(place, slashes, counts, query, parts):
    group = (1, GROUP) + SQUARE
    spec = pl.BlockSpec(group, lambda i: (i, 0, 0, 0))
    state = jax.ShapeDtypeStruct((Z_CHIPS, GROUP) + SQUARE, jnp.float32)
    return pl.pallas_call(
        near_kernel,
        out_shape=[state, state],
        grid=(Z_CHIPS,),
        in_specs=scalars(3) + [spec] + [pl.BlockSpec(memory_space=pl.ANY)] * (2 * PARTS),
        out_specs=[spec, spec],
        scratch_shapes=[
            pltpu.VMEM((2 * SEG_BLOCKS, 2) + SQUARE, jnp.bfloat16),
            pltpu.VMEM((2, GROUP, BLOCK_TOKENS, 2 * BLOCK_TOKENS), jnp.float32),
            pltpu.VMEM((GROUP,) + SQUARE, jnp.float32),
            pltpu.VMEM((GROUP,) + SQUARE, jnp.float32),
            pltpu.SemaphoreType.DMA((2 * PARTS,)),
        ],
        name="near_part",
    )(place, slashes, counts, query, *parts)


def far_kernel(
    place_ref,
    vertical_ref,
    slash_ref,
    count_ref,
    query_ref,
    mix_ref,
    stat_ref,
    pool,
    out_ref,
    score_ref,
    top_ref,
    total_ref,
    sum_ref,
):
    step = pl.program_id(0)
    segment, x_index, head = place_ref[0], place_ref[1], place_ref[2]
    used = count_ref[head, 0]
    pairs = (used + 1) >> 1
    turns = [(x_index - at) & (X_CHIPS - 1) for at in range(GROUP)]

    def active(slot, at):
        column = vertical_ref[head, slot]
        distance = segment * SEG_BLOCKS + turns[at] * Z_CHIPS + step - column
        keep = (slot < used) & (distance > 0)
        for which in range(NS):
            keep &= (which >= count_ref[head, 1]) | (distance != slash_ref[head, which])
        return bias_of(keep)

    for at in range(GROUP):
        top_ref[at] = jnp.broadcast_to(stat_ref[0, at, :, :1], SQUARE)

    def score(pair, carry):
        keys = two_blocks(pool, 2 * pair, 2 * pair + 1, 0)
        for at in range(GROUP):
            found = scores_of(query_ref[0, at], keys)
            left = found[:, :BLOCK_TOKENS] + active(2 * pair, at)
            right = found[:, BLOCK_TOKENS:] + active(2 * pair + 1, at)
            top_ref[at] = jnp.maximum(top_ref[at], jnp.maximum(left, right))
            score_ref[pair, at, :, :BLOCK_TOKENS] = left
            score_ref[pair, at, :, BLOCK_TOKENS:] = right
        return carry

    lax.fori_loop(0, pairs, score, 0)
    for at in range(GROUP):
        top = wide_top(top_ref[at])
        shrink = jnp.exp2((jnp.broadcast_to(stat_ref[0, at, :, :1], SQUARE) - top) * SCALE)
        top_ref[at] = top
        half = BLOCK_TOKENS // 2
        before = jnp.broadcast_to(stat_ref[0, at, :, half : half + 1], SQUARE)
        total_ref[at] = before * shrink * (1.0 / BLOCK_TOKENS)
        sum_ref[at] = mix_ref[0, at] * shrink

    def mix(pair, carry):
        values = two_blocks(pool, 2 * pair, 2 * pair + 1, 1)
        for at in range(GROUP):
            weights, total = weigh(score_ref, top_ref, pair, at)
            total_ref[at] += total
            sum_ref[at] += jnp.dot(weights, values, preferred_element_type=jnp.float32)
        return carry

    lax.fori_loop(0, pairs, mix, 0)
    for at in range(GROUP):
        total = jnp.sum(total_ref[at], axis=1, keepdims=True)
        out_ref[turns[at], 0] = (sum_ref[at] / total).astype(out_ref.dtype)


def far_part(place, verticals, slashes, counts, query, mixed, stats, columns):
    spec = pl.BlockSpec((1, GROUP) + SQUARE, lambda i: (i, 0, 0, 0))
    return pl.pallas_call(
        far_kernel,
        out_shape=jax.ShapeDtypeStruct((X_CHIPS, Z_CHIPS) + SQUARE, jnp.bfloat16),
        grid=(Z_CHIPS,),
        in_specs=scalars(4)
        + [spec] * 3
        + [pl.BlockSpec((NV, 2) + SQUARE, lambda i: (0, 0, 0, 0))],
        out_specs=pl.BlockSpec((X_CHIPS, 1) + SQUARE, lambda i: (0, i, 0, 0)),
        scratch_shapes=[
            pltpu.VMEM((NV // 2, GROUP, BLOCK_TOKENS, 2 * BLOCK_TOKENS), jnp.float32),
            pltpu.VMEM((GROUP,) + SQUARE, jnp.float32),
            pltpu.VMEM((GROUP,) + SQUARE, jnp.float32),
            pltpu.VMEM((GROUP,) + SQUARE, jnp.float32),
        ],
        name="far_part",
    )(place, verticals, slashes, counts, query, mixed, stats, columns)


def swapped(value, axes):
    return lax.all_to_all(value, axes, split_axis=0, concat_axis=0, tiled=True)


def shards(queries, key_row_matrix, values, verticals, slashes, counts):
    segment = lax.axis_index("seq")
    x_index = lax.axis_index("x")
    head = lax.axis_index("z") * X_CHIPS + x_index
    place = jnp.stack([segment, x_index, head]).astype(jnp.int32)

    both = packed(key_row_matrix[0], values[0])
    row = swapped(both, "z")
    hands = dealt(place, queries[0])
    hands = [hands[0]] + [
        shifted(hands[turn], "x", turn, X_CHIPS, True) for turn in range(1, X_CHIPS)
    ]
    hand = jnp.stack(hands, axis=1)
    query = swapped(hand, "z")

    after = shifted(row, "x", 1, X_CHIPS, True)
    before = shifted(row, "x", X_CHIPS - 1, X_CHIPS, True)
    earlier0 = shifted(row, "seq", 1, SEGMENTS, False)
    half = Z_CHIPS // 2
    across = [
        shifted(after[:half], "x", 1, X_CHIPS, True),
        shifted(before[half:], "x", X_CHIPS - 1, X_CHIPS, True),
    ]
    earlier1 = shifted(after, "seq", 1, SEGMENTS, False)
    earlier3 = shifted(before, "seq", 1, SEGMENTS, False)
    earlier2 = [shifted(part, "seq", 1, SEGMENTS, False) for part in across]
    rows = [row, after] + across + [before]
    earlier = [earlier0, earlier1] + earlier2 + [earlier3]

    mine = own_columns(place, verticals, rows)
    chunk = (SEGMENTS, NV * 2 * BLOCK_TOKENS // SEGMENTS, HEAD_WIDTH)
    pieces = swapped(mine.reshape(chunk), "seq")
    piece = pieces.astype(jnp.float32).sum(0).astype(jnp.bfloat16)
    wide = jnp.broadcast_to(piece[None], chunk)
    found = swapped(wide, "seq")
    found = found.reshape((NV, 2) + SQUARE)

    mixed, stats = near_part(place, slashes, counts, query, earlier + rows)
    context = far_part(place, verticals, slashes, counts, query, mixed, stats, found)
    back = swapped(context.reshape((QUERY_HEADS,) + SQUARE), ("x", "z"))
    back = back.reshape((X_CHIPS, Z_CHIPS) + SQUARE).transpose(2, 1, 0, 3)
    return back.reshape(1, BLOCK_TOKENS, QUERY_HEADS * HEAD_WIDTH)


def solution(mesh):
    fine = Mesh(mesh.devices.reshape(X_CHIPS, Z_CHIPS, SEGMENTS), ("x", "z", "seq"))
    spread = P("seq", ("x", "z"), None)
    return jax.shard_map(
        shards,
        mesh=fine,
        in_specs=(spread, spread, spread, P(), P(), P()),
        out_specs=spread,
        check_vma=False,
    )
```

time: 218 us -> 237 us (1.087)
  Pallas kernels: 14.3 us -> 30.6 us
  waiting for transfers between devices: 57.1 us -> 69.7 us
  starting transfers between devices: 46.5 us -> 53.9 us
  other arithmetic: 8.4 us -> 2.77 us
  blocking collectives: 77.2 us -> 71.7 us
  local copies, waits for them, and re-layouts: 11.8 us -> 6.89 us
    ppermute x9 -> x12, waiting for transfers between devices: 23.8 us -> 41.6 us  [shifted(): return lax.ppermute(value, axis, pairs)]
    pallas_call x2 -> x5, Pallas kernels: 14.3 us -> 30.6 us  [the longest x1 11.6 us: far_part(): pl.pallas_call(far_kernel, out_shape=jax.ShapeDtypeStruct((X_CHIPS, Z_CHI...]
    ppermute x9 -> x12, starting transfers between devices: 28.1 us -> 37.1 us  [shifted(): return lax.ppermute(value, axis, pairs)]
    all_to_all x2, blocking collectives: 77.2 us -> 71.7 us  [swapped(): return lax.all_to_all(value, axes, split_axis=0, concat_axis=0, tiled=True)]
    all_to_all x3, waiting for transfers between devices: 33.4 us -> 28.1 us  [swapped(): return lax.all_to_all(value, axes, split_axis=0, concat_axis=0, tiled=True)]
    and x2 -> x0, other arithmetic: 2.97 us -> none  [the longest x1 1.85 us: slot_tables(): is_column = (column_slot >= 0) & (column_slot < in_use[0])]
    another operation x0 -> x2, other arithmetic: none -> 2.71 us  [the longest x1 2.05 us: shards(): hand = jnp.stack(hands, axis=1)]
    select_n x3 -> x0, other arithmetic: 2.48 us -> none  [the longest x1 1.24 us: slot_tables(): bias = jnp.where(active, 0.0, -jnp.inf).astype(jnp.float32)]
  transfers between devices with their start and end apart: 12 -> 15, of which waited for: 7 -> 9; matrix products, arithmetic and copies ran while one was open for 5% -> 2% of each run, Pallas kernels for 0% -> 6%
where the time goes in v1:
time: 237 us; the launch traced here: 236 us
  blocking collectives  71.7 us (30%)
  waiting for transfers between devices  69.7 us (29%)
  starting transfers between devices  53.9 us (23%)
  Pallas kernels  30.6 us (13%)
  local copies, waits for them, and re-layouts  6.89 us (3%)
  other arithmetic  2.77 us (1%)
    all_to_all x2, blocking collectives, swapped(): return lax.all_to_all(value, axes, split_axis=0, concat_axis=0, tiled=True)  71.7 us
    ppermute x12, waiting for transfers between devices, shifted(): return lax.ppermute(value, axis, pairs)  41.6 us
    ppermute x12, starting transfers between devices, shifted(): return lax.ppermute(value, axis, pairs)  37.1 us
    all_to_all x3, waiting for transfers between devices, swapped(): return lax.all_to_all(value, axes, split_axis=0, concat_axis=0, tiled=True)  28.1 us
    all_to_all x3, starting transfers between devices, swapped(): return lax.all_to_all(value, axes, split_axis=0, concat_axis=0, tiled=True)  16.9 us
    pallas_call x1, Pallas kernels, far_part(): pl.pallas_call(far_kernel, out_shape=jax.ShapeDtypeStruct((X_CHIPS, Z_CHI...  11.6 us
    pallas_call x1, Pallas kernels, near_part(): pl.pallas_call(near_kernel, out_shape=[state, state], grid=(Z_CHIPS,), in...  11 us
  transfers between devices with their start and end apart: 15, of which 9 were waited for; matrix products, arithmetic and copies ran while one was open for 2% of the time, Pallas kernels for 6%

profile of v1, /device:TPU:16, one launch (start us, length us, event | category | flops | bytes accessed | tf_op | source)
XLA Modules:
  0.0 235.9 jit_solution(6447418351828031069)
XLA Ops:
  0.0 1.9 packed.1
  1.9 27.8 %all_to_all.25.refs_5_.refs_0_ = bf16[8,2,128,128]{3,2,1,0:T(8,128)(2,1)S(1)} all-to-all(bf16[8,2,128,128]{3,2,1,0:T(8,128)(2,1)} %packed.1), channel_id=1, replica_groups=mesh['x'=4,'z'=8,'seq'=16] {'z'}, dimensions={0} | all-to-all | bytes 1048576 | tf_op jit(solution)/shard_map/all_to_all | solution.py:333
  29.7 4.7 %collective-permute-start.8 = (bf16[8,2,128,128]{3,2,1,0:T(8,128)(2,1)S(1)}, bf16[8,2,128,128]{3,2,1,0:T(8,128)(2,1)S(1)}, u32[]{:S(2)}, u32[]{:S(2)}) collective-permute-start(bf16[8,2,128,128]{3,2,1,0:T(8,128)(2,1)S(1)} %all_to_all.25.refs_5_.refs_0_), channel_id=1, source_target_pairs={{0,384},{128,0},{256,128},{384,256},{1,385},{129,1},{257,129},{385... | collective-permute-start | bytes 1572872 | tf_op jit(solution)/shard_map/ppermute | solution.py:32
  34.4 1.9 collective-permute-start.4
  36.3 7.6 %collective-permute-done.8.refs_9_.refs_4_ = bf16[8,2,128,128]{3,2,1,0:T(8,128)(2,1)S(1)} collective-permute-done((bf16[8,2,128,128]{3,2,1,0:T(8,128)(2,1)S(1)}, bf16[8,2,128,128]{3,2,1,0:T(8,128)(2,1)S(1)}, u32[]{:S(2)}, u32[]{:S(2)}) %collective-permute-start.8) | collective-permute-done | bytes 524320 | tf_op jit(solution)/shard_map/ppermute | solution.py:32
  43.9 5.6 %collective-permute-start.9 = (bf16[4,2,128,128]{3,2,1,0:T(8,128)(2,1)S(1)}, bf16[4,2,128,128]{3,2,1,0:T(8,128)(2,1)S(1)}, u32[]{:S(2)}, u32[]{:S(2)}) collective-permute-start(bf16[4,2,128,128]{3,2,1,0:T(8,128)(2,1)S(1)} %slice.9), channel_id=1, source_target_pairs={{0,384},{128,0},{256,128},{384,256},{1,385},{129,1},{257,129},{385... | collective-permute-start | bytes 786440 | tf_op jit(solution)/shard_map/ppermute | solution.py:32
  49.5 0.0 collective-permute-done.4.refs_6_.refs_1_
  49.6 1.9 collective-permute-start.6
  51.5 0.7 copy.10.vertical_ref
  52.2 0.7 pad_add_fusion.place_ref
  52.9 0.5 collective-permute-done.9.refs_8_.refs_3_
  53.4 5.7 %collective-permute-done.6.refs_7_.refs_2_ = bf16[4,2,128,128]{3,2,1,0:T(8,128)(2,1)S(1)} collective-permute-done((bf16[4,2,128,128]{3,2,1,0:T(8,128)(2,1)S(1)}, bf16[4,2,128,128]{3,2,1,0:T(8,128)(2,1)S(1)}, u32[]{:S(2)}, u32[]{:S(2)}) %collective-permute-start.6) | collective-permute-done | bytes 262176 | tf_op jit(solution)/shard_map/ppermute | solution.py:32
  59.1 0.7 copy-done.10
  59.8 3.5 %own_columns.1 = bf16[6,2,128,128]{3,2,1,0:T(8,128)(2,1)} custom-call(s32[3]{0:T(128)} %pad_add_fusion.place_ref, s32[32,6]{1,0:T(8,128)} %copy.10.vertical_ref, bf16[8,2,128,128]{3,2,1,0:T(8,128)(2,1)} %copy-done.1, bf16[8,2,128,128]{3,2,1,0:T(8,128)(2,1)} %copy-done.5, bf16[4,2,128,128]{3,2,1,0:T(8,128)(2,1)} %copy-done.10, ...), custom_call_target="tpu_custom_call" | custom-call | tf_op jit(solution)/shard_map/own_columns/pallas_call | solution.py:102
  63.4 5.9 %all-to-all-start.2 = ((bf16[16,96,128]{2,1,0:T(8,128)(2,1)}), bf16[16,96,128]{2,1,0:T(8,128)(2,1)S(1)}, u32[]{:S(2)}, u32[]{:S(2)}) async-start(bf16[16,96,128]{2,1,0:T(8,128)(2,1)} %bitcast.20), calls=%async_computation.2 | async-start | bytes 786432 | tf_op jit(solution)/shard_map/all_to_all | solution.py:333
  69.3 2.5 %dealt.1 = (bf16[8,128,128]{2,1,0:T(8,128)(2,1)}, bf16[8,128,128]{2,1,0:T(8,128)(2,1)}, bf16[8,128,128]{2,1,0:T(8,128)(2,1)}, bf16[8,128,128]{2,1,0:T(8,128)(2,1)}) custom-call(s32[3]{0:T(128)} %pad_add_fusion.place_ref, bf16[128,4096]{1,0:T(8,128)(2,1)} %bitcast.22), custom_call_target="tpu_custom_call" | custom-call | tf_op jit(solution)/shard_map/dealt/pallas_call | solution.py:65
  71.8 1.9 collective-permute-start
  73.7 2.8 %collective-permute-start.1 = (bf16[8,128,128]{2,1,0:T(8,128)(2,1)}, bf16[8,128,128]{2,1,0:T(8,128)(2,1)S(1)}, u32[]{:S(2)}, u32[]{:S(2)}) collective-permute-start(bf16[8,128,128]{2,1,0:T(8,128)(2,1)} %get-tuple-element.13), channel_id=1, source_target_pairs={{0,256},{128,384},{256,0},{384,128},{1,257},{129,385},{257,1},{385... | collective-permute-start | bytes 786440 | tf_op jit(solution)/shard_map/ppermute | solution.py:32
  76.6 4.2 %collective-permute-start.2 = (bf16[8,128,128]{2,1,0:T(8,128)(2,1)}, bf16[8,128,128]{2,1,0:T(8,128)(2,1)S(1)}, u32[]{:S(2)}, u32[]{:S(2)}) collective-permute-start(bf16[8,128,128]{2,1,0:T(8,128)(2,1)} %get-tuple-element.14), channel_id=1, source_target_pairs={{0,384},{128,0},{256,128},{384,256},{1,385},{129,1},{257,129},{385... | collective-permute-start | bytes 786440 | tf_op jit(solution)/shard_map/ppermute | solution.py:32
  80.8 8.3 %collective-permute-done = bf16[8,128,128]{2,1,0:T(8,128)(2,1)S(1)} collective-permute-done((bf16[8,128,128]{2,1,0:T(8,128)(2,1)}, bf16[8,128,128]{2,1,0:T(8,128)(2,1)S(1)}, u32[]{:S(2)}, u32[]{:S(2)}) %collective-permute-start) | collective-permute-done | bytes 262176 | tf_op jit(solution)/shard_map/ppermute | solution.py:32
  89.0 0.0 collective-permute-done.1
  89.0 2.5 %collective-permute-done.2 = bf16[8,128,128]{2,1,0:T(8,128)(2,1)S(1)} collective-permute-done((bf16[8,128,128]{2,1,0:T(8,128)(2,1)}, bf16[8,128,128]{2,1,0:T(8,128)(2,1)S(1)}, u32[]{:S(2)}, u32[]{:S(2)}) %collective-permute-start.2) | collective-permute-done | bytes 262176 | tf_op jit(solution)/shard_map/ppermute | solution.py:32
  91.6 2.0 pad_maximum_fusion
  93.6 0.0 copy-start.12
  93.6 0.0 copy-start.13
  93.6 0.0 all-to-all-done.2
  93.7 3.7 %all-to-all-start = ((bf16[8,4,128,128]{3,2,1,0:T(8,128)(2,1)}), bf16[8,4,128,128]{3,2,1,0:T(8,128)(2,1)S(1)}, u32[]{:S(2)}, u32[]{:S(2)}) async-start(bf16[8,4,128,128]{3,2,1,0:T(8,128)(2,1)} %pad_maximum_fusion), calls=%async_computation | async-start | bytes 2097152 | tf_op jit(solution)/shard_map/all_to_all | solution.py:333
  97.4 0.1 reduce_sum.12
  97.4 28.1 %all-to-all-done.query_ref = bf16[8,4,128,128]{3,2,1,0:T(8,128)(2,1)S(1)} async-done(((bf16[8,4,128,128]{3,2,1,0:T(8,128)(2,1)}), bf16[8,4,128,128]{3,2,1,0:T(8,128)(2,1)S(1)}, u32[]{:S(2)}, u32[]{:S(2)}) %all-to-all-start) | async-done | bytes 1048608 | tf_op jit(solution)/shard_map/all_to_all | solution.py:333
  125.5 0.9 broadcast_in_dim.2
  126.4 7.2 %all-to-all-start.3 = ((bf16[16,96,128]{2,1,0:T(8,128)(2,1)}), bf16[16,96,128]{2,1,0:T(8,128)(2,1)S(1)}, u32[]{:S(2)}, u32[]{:S(2)}) async-start(bf16[16,96,128]{2,1,0:T(8,128)(2,1)} %broadcast_in_dim.2), calls=%async_computation.3 | async-start | bytes 786432 | tf_op jit(solution)/shard_map/all_to_all | solution.py:333
  133.6 2.0 collective-permute-start.3
  135.6 3.4 %collective-permute-start.11 = (bf16[8,2,128,128]{3,2,1,0:T(8,128)(2,1)S(1)}, bf16[8,2,128,128]{3,2,1,0:T(8,128)(2,1)}, u32[]{:S(2)}, u32[]{:S(2)}) collective-permute-start(bf16[8,2,128,128]{3,2,1,0:T(8,128)(2,1)S(1)} %copy-done.4), channel_id=1, source_target_pairs={{0,1},{1,2},{2,3},{3,4},{4,5},{5,6},{6,7},{7,8},{8,9},{9,10},{10,1... | collective-permute-start | bytes 1572872 | tf_op jit(solution)/shard_map/ppermute | solution.py:32
  139.0 2.0 collective-permute-start.5
  141.1 4.6 %collective-permute-start.10 = (bf16[4,2,128,128]{3,2,1,0:T(8,128)(2,1)S(1)}, bf16[4,2,128,128]{3,2,1,0:T(8,128)(2,1)}, u32[]{:S(2)}, u32[]{:S(2)}) collective-permute-start(bf16[4,2,128,128]{3,2,1,0:T(8,128)(2,1)S(1)} %copy-done.9), channel_id=1, source_target_pairs={{0,1},{1,2},{2,3},{3,4},{4,5},{5,6},{6,7},{7,8},{8,9},{9,10},{10,1... | collective-permute-start | bytes 786440 | tf_op jit(solution)/shard_map/ppermute | solution.py:32
  145.7 2.0 collective-permute-start.7
  147.7 0.7 copy.11.slash_ref
  148.4 0.7 copy.12.count_ref
  149.1 0.2 collective-permute-done.3.refs_0_
  149.3 14.0 %collective-permute-done.10.refs_3_ = bf16[4,2,128,128]{3,2,1,0:T(8,128)(2,1)} collective-permute-done((bf16[4,2,128,128]{3,2,1,0:T(8,128)(2,1)S(1)}, bf16[4,2,128,128]{3,2,1,0:T(8,128)(2,1)}, u32[]{:S(2)}, u32[]{:S(2)}) %collective-permute-start.10) | collective-permute-done | bytes 262176 | tf_op jit(solution)/shard_map/ppermute | solution.py:32
  163.3 2.8 %collective-permute-done.7.refs_2_ = bf16[4,2,128,128]{3,2,1,0:T(8,128)(2,1)} collective-permute-done((bf16[4,2,128,128]{3,2,1,0:T(8,128)(2,1)}, bf16[4,2,128,128]{3,2,1,0:T(8,128)(2,1)}, u32[]{:S(2)}, u32[]{:S(2)}) %collective-permute-start.7) | collective-permute-done | bytes 262176 | tf_op jit(solution)/shard_map/ppermute | solution.py:32
  166.2 11.0 %near_part.1 = (f32[8,4,128,128]{3,2,1,0:T(8,128)}, f32[8,4,128,128]{3,2,1,0:T(8,128)}) custom-call(s32[3]{0:T(128)} %pad_add_fusion.place_ref, s32[32,3]{1,0:T(8,128)} %copy.11.slash_ref, s32[32,2]{1,0:T(8,128)} %copy.12.count_ref, bf16[8,4,128,128]{3,2,1,0:T(8,128)(2,1)} %copy-done, bf16[8,2,128,128]{3,2,1,0:T(8,128)(2,1)} %collective-permute-done.3.refs_0_, ...), custom_call_target="tpu_custom_call" | custom-call | tf_op jit(solution)/shard_map/near_part/pallas_call | solution.py:228
  177.2 0.0 all-to-all-done.3
  177.2 0.7 copy-done.7
  177.9 11.6 %far_part.1 = bf16[4,8,128,128]{3,2,1,0:T(8,128)(2,1)} custom-call(s32[3]{0:T(128)} %pad_add_fusion.place_ref, s32[32,6]{1,0:T(8,128)} %copy.10.vertical_ref, s32[32,3]{1,0:T(8,128)} %copy.11.slash_ref, s32[32,2]{1,0:T(8,128)} %copy.12.count_ref, bf16[8,4,128,128]{3,2,1,0:T(8,128)(2,1)} %copy-done, f32[8,4,128,128]{3,2,1,0:T(8,128)} %get-tuple-element.15.mix_ref, ...), custom_call_target="tpu_custom_call" | custom-call | tf_op jit(solution)/shard_map/far_part/pallas_call | solution.py:314
  189.6 43.9 %all_to_all.26 = bf16[32,128,128]{2,1,0:T(8,128)(2,1)S(1)} all-to-all(bf16[32,128,128]{2,1,0:T(8,128)(2,1)} %bitcast.19), channel_id=1, replica_groups=mesh['x'=4,'z'=8,'seq'=16] {'x','z'}, dimensions={0} | all-to-all | bytes 2097152 | tf_op jit(solution)/shard_map/all_to_all | solution.py:333
  233.5 0.8 copy.15
  234.3 1.6 reshape.20
  (28 shorter events, 0.1 us)
Async XLA Ops:
  0.0 51.5 %copy-start.11 = (s32[32,6]{0,1:T(8,128)S(1)}, s32[32,6]{0,1:T(8,128)}, u32[]{:S(2)}) copy-start(s32[32,6]{0,1:T(8,128)} %param.9) | copy-start | bytes 2308
  29.7 29.3 %copy-start.1 = (bf16[8,2,128,128]{3,2,1,0:T(8,128)(2,1)}, bf16[8,2,128,128]{3,2,1,0:T(8,128)(2,1)S(1)}, u32[]{:S(2)}) copy-start(bf16[8,2,128,128]{3,2,1,0:T(8,128)(2,1)S(1)} %all_to_all.25.refs_5_.refs_0_) | copy-start | bytes 1572868
  29.7 14.2 %collective-permute-start.8 = (bf16[8,2,128,128]{3,2,1,0:T(8,128)(2,1)S(1)}, bf16[8,2,128,128]{3,2,1,0:T(8,128)(2,1)S(1)}, u32[]{:S(2)}, u32[]{:S(2)}) collective-permute-start(bf16[8,2,128,128]{3,2,1,0:T(8,128)(2,1)S(1)} %all_to_all.25.refs_5_.refs_0_), channel_id=1, source_target_pairs={{0,384},{128,0},{256,128},{384,256},{1,385},{129,1},{257,129},{385... | collective-permute-start | bytes 1572872 | tf_op jit(solution)/shard_map/ppermute | solution.py:32
  34.4 15.1 %collective-permute-start.4 = (bf16[8,2,128,128]{3,2,1,0:T(8,128)(2,1)S(1)}, bf16[8,2,128,128]{3,2,1,0:T(8,128)(2,1)S(1)}, u32[]{:S(2)}, u32[]{:S(2)}) collective-permute-start(bf16[8,2,128,128]{3,2,1,0:T(8,128)(2,1)S(1)} %all_to_all.25.refs_5_.refs_0_), channel_id=1, source_target_pairs={{0,128},{128,256},{256,384},{384,0},{1,129},{129,257},{257,385},{3... | collective-permute-start | bytes 1572872 | tf_op jit(solution)/shard_map/ppermute | solution.py:32
  43.9 15.2 %copy-start.3 = (bf16[8,2,128,128]{3,2,1,0:T(8,128)(2,1)}, bf16[8,2,128,128]{3,2,1,0:T(8,128)(2,1)S(1)}, u32[]{:S(2)}) copy-start(bf16[8,2,128,128]{3,2,1,0:T(8,128)(2,1)S(1)} %collective-permute-done.8.refs_9_.refs_4_) | copy-start | bytes 1572868
  43.9 9.5 %collective-permute-start.9 = (bf16[4,2,128,128]{3,2,1,0:T(8,128)(2,1)S(1)}, bf16[4,2,128,128]{3,2,1,0:T(8,128)(2,1)S(1)}, u32[]{:S(2)}, u32[]{:S(2)}) collective-permute-start(bf16[4,2,128,128]{3,2,1,0:T(8,128)(2,1)S(1)} %slice.9), channel_id=1, source_target_pairs={{0,384},{128,0},{256,128},{384,256},{1,385},{129,1},{257,129},{385... | collective-permute-start | bytes 786440 | tf_op jit(solution)/shard_map/ppermute | solution.py:32
  49.5 9.5 %copy-start.5 = (bf16[8,2,128,128]{3,2,1,0:T(8,128)(2,1)}, bf16[8,2,128,128]{3,2,1,0:T(8,128)(2,1)S(1)}, u32[]{:S(2)}) copy-start(bf16[8,2,128,128]{3,2,1,0:T(8,128)(2,1)S(1)} %collective-permute-done.4.refs_6_.refs_1_) | copy-start | bytes 1572868
  49.6 9.5 %collective-permute-start.6 = (bf16[4,2,128,128]{3,2,1,0:T(8,128)(2,1)S(1)}, bf16[4,2,128,128]{3,2,1,0:T(8,128)(2,1)S(1)}, u32[]{:S(2)}, u32[]{:S(2)}) collective-permute-start(bf16[4,2,128,128]{3,2,1,0:T(8,128)(2,1)S(1)} %slice.8), channel_id=1, source_target_pairs={{0,128},{128,256},{256,384},{384,0},{1,129},{129,257},{257,385},{3... | collective-permute-start | bytes 786440 | tf_op jit(solution)/shard_map/ppermute | solution.py:32
  53.4 5.7 %copy-start.8 = (bf16[4,2,128,128]{3,2,1,0:T(8,128)(2,1)}, bf16[4,2,128,128]{3,2,1,0:T(8,128)(2,1)S(1)}, u32[]{:S(2)}) copy-start(bf16[4,2,128,128]{3,2,1,0:T(8,128)(2,1)S(1)} %collective-permute-done.9.refs_8_.refs_3_) | copy-start | bytes 786436
  59.1 0.7 copy-start.10
  63.4 30.3 %all-to-all-start.2 = ((bf16[16,96,128]{2,1,0:T(8,128)(2,1)}), bf16[16,96,128]{2,1,0:T(8,128)(2,1)S(1)}, u32[]{:S(2)}, u32[]{:S(2)}) async-start(bf16[16,96,128]{2,1,0:T(8,128)(2,1)} %bitcast.20), calls=%async_computation.2 | async-start | bytes 786432 | tf_op jit(solution)/shard_map/all_to_all | solution.py:333
  71.8 17.2 %collective-permute-start = (bf16[8,128,128]{2,1,0:T(8,128)(2,1)}, bf16[8,128,128]{2,1,0:T(8,128)(2,1)S(1)}, u32[]{:S(2)}, u32[]{:S(2)}) collective-permute-start(bf16[8,128,128]{2,1,0:T(8,128)(2,1)} %get-tuple-element.12), channel_id=1, source_target_pairs={{0,128},{128,256},{256,384},{384,0},{1,129},{129,257},{257,385},{3... | collective-permute-start | bytes 786440 | tf_op jit(solution)/shard_map/ppermute | solution.py:32
  73.7 15.3 %collective-permute-start.1 = (bf16[8,128,128]{2,1,0:T(8,128)(2,1)}, bf16[8,128,128]{2,1,0:T(8,128)(2,1)S(1)}, u32[]{:S(2)}, u32[]{:S(2)}) collective-permute-start(bf16[8,128,128]{2,1,0:T(8,128)(2,1)} %get-tuple-element.13), channel_id=1, source_target_pairs={{0,256},{128,384},{256,0},{384,128},{1,257},{129,385},{257,1},{385... | collective-permute-start | bytes 786440 | tf_op jit(solution)/shard_map/ppermute | solution.py:32
  76.6 15.0 %collective-permute-start.2 = (bf16[8,128,128]{2,1,0:T(8,128)(2,1)}, bf16[8,128,128]{2,1,0:T(8,128)(2,1)S(1)}, u32[]{:S(2)}, u32[]{:S(2)}) collective-permute-start(bf16[8,128,128]{2,1,0:T(8,128)(2,1)} %get-tuple-element.14), channel_id=1, source_target_pairs={{0,384},{128,0},{256,128},{384,256},{1,385},{129,1},{257,129},{385... | collective-permute-start | bytes 786440 | tf_op jit(solution)/shard_map/ppermute | solution.py:32
  93.6 40.0 %copy-start.2 = (bf16[8,2,128,128]{3,2,1,0:T(8,128)(2,1)S(1)}, bf16[8,2,128,128]{3,2,1,0:T(8,128)(2,1)}, u32[]{:S(2)}) copy-start(bf16[8,2,128,128]{3,2,1,0:T(8,128)(2,1)} %copy-done.1) | copy-start | bytes 1572868
  93.6 42.0 %copy-start.4 = (bf16[8,2,128,128]{3,2,1,0:T(8,128)(2,1)S(1)}, bf16[8,2,128,128]{3,2,1,0:T(8,128)(2,1)}, u32[]{:S(2)}) copy-start(bf16[8,2,128,128]{3,2,1,0:T(8,128)(2,1)} %copy-done.3) | copy-start | bytes 1572868
  93.6 45.4 %copy-start.6 = (bf16[8,2,128,128]{3,2,1,0:T(8,128)(2,1)S(1)}, bf16[8,2,128,128]{3,2,1,0:T(8,128)(2,1)}, u32[]{:S(2)}) copy-start(bf16[8,2,128,128]{3,2,1,0:T(8,128)(2,1)} %copy-done.5) | copy-start | bytes 1572868
  93.6 47.5 %copy-start.9 = (bf16[4,2,128,128]{3,2,1,0:T(8,128)(2,1)S(1)}, bf16[4,2,128,128]{3,2,1,0:T(8,128)(2,1)}, u32[]{:S(2)}) copy-start(bf16[4,2,128,128]{3,2,1,0:T(8,128)(2,1)} %copy-done.8) | copy-start | bytes 786436
  93.6 54.1 %copy-start.12 = (s32[32,3]{0,1:T(4,128)S(1)}, s32[32,3]{0,1:T(4,128)}, u32[]{:S(2)}) copy-start(s32[32,3]{0,1:T(4,128)} %param.10) | copy-start | bytes 1156
  93.6 54.8 %copy-start.13 = (s32[32,2]{0,1:T(2,128)S(1)}, s32[32,2]{0,1:T(2,128)}, u32[]{:S(2)}) copy-start(s32[32,2]{0,1:T(2,128)} %param.11) | copy-start | bytes 772
  93.7 31.9 %all-to-all-start = ((bf16[8,4,128,128]{3,2,1,0:T(8,128)(2,1)}), bf16[8,4,128,128]{3,2,1,0:T(8,128)(2,1)S(1)}, u32[]{:S(2)}, u32[]{:S(2)}) async-start(bf16[8,4,128,128]{3,2,1,0:T(8,128)(2,1)} %pad_maximum_fusion), calls=%async_computation | async-start | bytes 2097152 | tf_op jit(solution)/shard_map/all_to_all | solution.py:333
  125.5 40.6 %copy-start = (bf16[8,4,128,128]{3,2,1,0:T(8,128)(2,1)}, bf16[8,4,128,128]{3,2,1,0:T(8,128)(2,1)S(1)}, u32[]{:S(2)}) copy-start(bf16[8,4,128,128]{3,2,1,0:T(8,128)(2,1)S(1)} %all-to-all-done.query_ref) | copy-start | bytes 3145732
  126.4 50.8 %all-to-all-start.3 = ((bf16[16,96,128]{2,1,0:T(8,128)(2,1)}), bf16[16,96,128]{2,1,0:T(8,128)(2,1)S(1)}, u32[]{:S(2)}, u32[]{:S(2)}) async-start(bf16[16,96,128]{2,1,0:T(8,128)(2,1)} %broadcast_in_dim.2), calls=%async_computation.3 | async-start | bytes 786432 | tf_op jit(solution)/shard_map/all_to_all | solution.py:333
  133.6 15.7 %collective-permute-start.3 = (bf16[8,2,128,128]{3,2,1,0:T(8,128)(2,1)S(1)}, bf16[8,2,128,128]{3,2,1,0:T(8,128)(2,1)}, u32[]{:S(2)}, u32[]{:S(2)}) collective-permute-start(bf16[8,2,128,128]{3,2,1,0:T(8,128)(2,1)S(1)} %copy-done.2), channel_id=1, source_target_pairs={{0,1},{1,2},{2,3},{3,4},{4,5},{5,6},{6,7},{7,8},{8,9},{9,10},{10,1... | collective-permute-start | bytes 1572872 | tf_op jit(solution)/shard_map/ppermute | solution.py:32
  135.6 30.5 %collective-permute-start.11 = (bf16[8,2,128,128]{3,2,1,0:T(8,128)(2,1)S(1)}, bf16[8,2,128,128]{3,2,1,0:T(8,128)(2,1)}, u32[]{:S(2)}, u32[]{:S(2)}) collective-permute-start(bf16[8,2,128,128]{3,2,1,0:T(8,128)(2,1)S(1)} %copy-done.4), channel_id=1, source_target_pairs={{0,1},{1,2},{2,3},{3,4},{4,5},{5,6},{6,7},{7,8},{8,9},{9,10},{10,1... | collective-permute-start | bytes 1572872 | tf_op jit(solution)/shard_map/ppermute | solution.py:32
  139.0 27.1 %collective-permute-start.5 = (bf16[8,2,128,128]{3,2,1,0:T(8,128)(2,1)S(1)}, bf16[8,2,128,128]{3,2,1,0:T(8,128)(2,1)}, u32[]{:S(2)}, u32[]{:S(2)}) collective-permute-start(bf16[8,2,128,128]{3,2,1,0:T(8,128)(2,1)S(1)} %copy-done.6), channel_id=1, source_target_pairs={{0,1},{1,2},{2,3},{3,4},{4,5},{5,6},{6,7},{7,8},{8,9},{9,10},{10,1... | collective-permute-start | bytes 1572872 | tf_op jit(solution)/shard_map/ppermute | solution.py:32
  141.1 22.3 %collective-permute-start.10 = (bf16[4,2,128,128]{3,2,1,0:T(8,128)(2,1)S(1)}, bf16[4,2,128,128]{3,2,1,0:T(8,128)(2,1)}, u32[]{:S(2)}, u32[]{:S(2)}) collective-permute-start(bf16[4,2,128,128]{3,2,1,0:T(8,128)(2,1)S(1)} %copy-done.9), channel_id=1, source_target_pairs={{0,1},{1,2},{2,3},{3,4},{4,5},{5,6},{6,7},{7,8},{8,9},{9,10},{10,1... | collective-permute-start | bytes 786440 | tf_op jit(solution)/shard_map/ppermute | solution.py:32
  145.7 20.5 %collective-permute-start.7 = (bf16[4,2,128,128]{3,2,1,0:T(8,128)(2,1)}, bf16[4,2,128,128]{3,2,1,0:T(8,128)(2,1)}, u32[]{:S(2)}, u32[]{:S(2)}) collective-permute-start(bf16[4,2,128,128]{3,2,1,0:T(8,128)(2,1)} %copy-done.10), channel_id=1, source_target_pairs={{0,1},{1,2},{2,3},{3,4},{4,5},{5,6},{6,7},{7,8},{8,9},{9,10},{10,1... | collective-permute-start | bytes 786440 | tf_op jit(solution)/shard_map/ppermute | solution.py:32
  177.2 0.7 copy-start.7

commit v2 on v1

v2 whole, which is shorter than its diff:
```python
import math

import jax
import jax.numpy as jnp
from jax import lax
from jax.experimental import pallas as pl
from jax.experimental.pallas import tpu as pltpu
from jax.sharding import Mesh
from jax.sharding import PartitionSpec as P


QUERY_HEADS = 32
KEY_VALUE_HEADS = 8
HEAD_WIDTH = 128
BLOCK_TOKENS = 128
X_CHIPS = 4
Z_CHIPS = 8
SEGMENTS = 16
NV = 6
NS = 3
SEG_BLOCKS = 32
GROUP = 16
ROW_BLOCKS = 8
STEPS = SEG_BLOCKS // GROUP

SCALE = math.log2(math.e) / math.sqrt(HEAD_WIDTH)
SQUARE = (BLOCK_TOKENS, HEAD_WIDTH)


def shifted(value, axis, distance, size, wrap):
    pairs = [(i, (i + distance) % size) for i in range(size) if wrap or i + distance < size]
    return lax.ppermute(value, axis, pairs)


def scalars(count):
    return [pl.BlockSpec(memory_space=pltpu.SMEM)] * count


def pack_kernel(key_ref, value_ref, out_ref):
    for head in range(KEY_VALUE_HEADS):
        lanes = slice(head * HEAD_WIDTH, (head + 1) * HEAD_WIDTH)
        out_ref[head, 0] = key_ref[:, lanes]
        out_ref[head, 1] = value_ref[:, lanes]


def packed(keys, values):
    return pl.pallas_call(
        pack_kernel,
        out_shape=jax.ShapeDtypeStruct((KEY_VALUE_HEADS, 2) + SQUARE, jnp.bfloat16),
        name="packed",
    )(keys, values)


def deal_kernel(query_ref, out_ref):
    for x_index in range(X_CHIPS):
        for z_index in range(Z_CHIPS):
            start = (z_index * X_CHIPS + x_index) * HEAD_WIDTH
            out_ref[x_index * Z_CHIPS + z_index] = query_ref[:, start : start + HEAD_WIDTH]


def dealt(query):
    return pl.pallas_call(
        deal_kernel,
        out_shape=jax.ShapeDtypeStruct((QUERY_HEADS,) + SQUARE, jnp.bfloat16),
        name="dealt",
    )(query)


def pool_index(source, x_index):
    row = source >> 3
    turn = (x_index - row) & (X_CHIPS - 1)
    return ((row >> 2) * X_CHIPS + turn) * ROW_BLOCKS + (source & (ROW_BLOCKS - 1))


def column_kernel(place_ref, vertical_ref, *refs):
    rows, (out_ref, sems) = refs[:X_CHIPS], refs[X_CHIPS:]
    out_ref[...] = jnp.zeros_like(out_ref)
    for slot in range(NV):
        column = vertical_ref[place_ref[1], slot]
        at = pool_index(column & (SEG_BLOCKS - 1), place_ref[2])
        mine = (column >> 5) == place_ref[0]
        for turn, row in enumerate(rows):

            @pl.when(mine & ((at >> 3) == turn))
            def _():
                copy = pltpu.make_async_copy(
                    row.at[at & (ROW_BLOCKS - 1)], out_ref.at[slot], sems.at[slot]
                )
                copy.start()
                copy.wait()


def own_columns(place, verticals, rows):
    return pl.pallas_call(
        column_kernel,
        out_shape=jax.ShapeDtypeStruct((NV, 2) + SQUARE, jnp.bfloat16),
        in_specs=scalars(2) + [pl.BlockSpec(memory_space=pl.ANY)] * X_CHIPS,
        out_specs=pl.BlockSpec(memory_space=pltpu.VMEM),
        scratch_shapes=[pltpu.SemaphoreType.DMA((NV,))],
        name="own_columns",
    )(place, verticals, *rows)


def two_blocks(pool, left, right, part):
    return jnp.concatenate([pool[left, part], pool[right, part]], axis=0)


def scores_of(query, keys):
    return lax.dot_general(
        query, keys, (((1,), (1,)), ((), ())), preferred_element_type=jnp.float32
    )


def weigh(score_ref, top_ref, pair, at):
    top = top_ref[at]
    top = jnp.concatenate([top, top], axis=1)
    weights = jnp.exp2((score_ref[pair, at] - top) * SCALE)
    total = weights[:, :BLOCK_TOKENS] + weights[:, BLOCK_TOKENS:]
    return weights.astype(jnp.bfloat16), total


def bias_of(active):
    return jnp.where(active, 0.0, -jnp.inf).astype(jnp.float32)


def wide_top(top):
    return jnp.broadcast_to(jnp.max(top, axis=1, keepdims=True), SQUARE)


def near_kernel(
    place_ref,
    slash_ref,
    count_ref,
    query_ref,
    *refs,
):
    rows = refs[: 2 * X_CHIPS]
    mix_ref, stat_ref, pool, score_ref, top_ref, total_ref, sems = refs[2 * X_CHIPS :]
    step = pl.program_id(0)
    segment, head, x_index = place_ref[0], place_ref[1], place_ref[2]
    used = count_ref[head, 1]
    pairs = (used + 2) >> 1

    @pl.when(step == 0)
    def _():
        copies = [
            pltpu.make_async_copy(row, pool.at[pl.ds(at * ROW_BLOCKS, ROW_BLOCKS)], sems.at[at])
            for at, row in enumerate(rows)
        ]
        for copy in copies:
            copy.start()
        for copy in copies:
            copy.wait()

    blocks = [step * GROUP + at for at in range(GROUP)]
    row_ids = lax.broadcasted_iota(jnp.int32, SQUARE, 0)
    col_ids = lax.broadcasted_iota(jnp.int32, SQUARE, 1)

    def offset_of(slot):
        live = slot <= used
        return jnp.where(live, slash_ref[head, jnp.clip(slot - 1, 0, NS - 1)], 0), live

    def place_of(offset, block):
        return pool_index(block - offset + SEG_BLOCKS, x_index)

    def score(pair, first):
        offsets = [(0, True) if first else offset_of(2 * pair), offset_of(2 * pair + 1)]
        for at, block in enumerate(blocks):
            spots = [place_of(offset, block) for offset, _ in offsets]
            found = scores_of(query_ref[at], two_blocks(pool, *spots, 0))
            reach = segment * SEG_BLOCKS + block
            right = found[:, BLOCK_TOKENS:] + bias_of(
                offsets[1][1] & (reach >= offsets[1][0])
            )
            left = found[:, :BLOCK_TOKENS]
            if first:
                left = jnp.where(row_ids >= col_ids, left, -jnp.inf)
                top_ref[at] = jnp.maximum(left, right)
            else:
                left = left + bias_of(offsets[0][1] & (reach >= offsets[0][0]))
                top_ref[at] = jnp.maximum(top_ref[at], jnp.maximum(left, right))
            score_ref[pair, at, :, :BLOCK_TOKENS] = left
            score_ref[pair, at, :, BLOCK_TOKENS:] = right

    def mix(pair, first):
        offsets = [0 if first else offset_of(2 * pair)[0], offset_of(2 * pair + 1)[0]]
        for at, block in enumerate(blocks):
            spots = [place_of(offset, block) for offset in offsets]
            weights, total = weigh(score_ref, top_ref, pair, at)
            mixed = jnp.dot(
                weights, two_blocks(pool, *spots, 1), preferred_element_type=jnp.float32
            )
            if first:
                total_ref[at] = total
                mix_ref[at] = mixed
            else:
                total_ref[at] += total
                mix_ref[at] += mixed

    score(0, True)

    @pl.when(pairs > 1)
    def _():
        score(1, False)

    for at in range(GROUP):
        top_ref[at] = wide_top(top_ref[at])
    mix(0, True)

    @pl.when(pairs > 1)
    def _():
        mix(1, False)

    for at in range(GROUP):
        total = jnp.sum(total_ref[at], axis=1, keepdims=True)
        stat_ref[at] = jnp.where(
            col_ids < BLOCK_TOKENS // 2, top_ref[at], jnp.broadcast_to(total, SQUARE)
        )


def near_part(place, slashes, counts, query, rows):
    spec = pl.BlockSpec((GROUP,) + SQUARE, lambda i: (i, 0, 0))
    state = jax.ShapeDtypeStruct((SEG_BLOCKS,) + SQUARE, jnp.float32)
    return pl.pallas_call(
        near_kernel,
        out_shape=[state, state],
        grid=(STEPS,),
        in_specs=scalars(3) + [spec] + [pl.BlockSpec(memory_space=pl.ANY)] * (2 * X_CHIPS),
        out_specs=[spec, spec],
        scratch_shapes=[
            pltpu.VMEM((2 * SEG_BLOCKS, 2) + SQUARE, jnp.bfloat16),
            pltpu.VMEM((2, GROUP, BLOCK_TOKENS, 2 * BLOCK_TOKENS), jnp.float32),
            pltpu.VMEM((GROUP,) + SQUARE, jnp.float32),
            pltpu.VMEM((GROUP,) + SQUARE, jnp.float32),
            pltpu.SemaphoreType.DMA((2 * X_CHIPS,)),
        ],
        name="near_part",
    )(place, slashes, counts, query, *rows)


def far_kernel(
    place_ref,
    vertical_ref,
    slash_ref,
    count_ref,
    query_ref,
    mix_ref,
    stat_ref,
    pool,
    out_ref,
    score_ref,
    top_ref,
    total_ref,
    sum_ref,
):
    step = pl.program_id(0)
    segment, head = place_ref[0], place_ref[1]
    used = count_ref[head, 0]
    pairs = (used + 1) >> 1

    def active(slot, at):
        column = vertical_ref[head, slot]
        distance = segment * SEG_BLOCKS + step * GROUP + at - column
        keep = (slot < used) & (distance > 0)
        for which in range(NS):
            keep &= (which >= count_ref[head, 1]) | (distance != slash_ref[head, which])
        return bias_of(keep)

    for at in range(GROUP):
        top_ref[at] = jnp.broadcast_to(stat_ref[at, :, :1], SQUARE)

    def score(pair, carry):
        keys = two_blocks(pool, 2 * pair, 2 * pair + 1, 0)
        for at in range(GROUP):
            found = scores_of(query_ref[at], keys)
            left = found[:, :BLOCK_TOKENS] + active(2 * pair, at)
            right = found[:, BLOCK_TOKENS:] + active(2 * pair + 1, at)
            top_ref[at] = jnp.maximum(top_ref[at], jnp.maximum(left, right))
            score_ref[pair, at, :, :BLOCK_TOKENS] = left
            score_ref[pair, at, :, BLOCK_TOKENS:] = right
        return carry

    lax.fori_loop(0, pairs, score, 0)
    for at in range(GROUP):
        top = wide_top(top_ref[at])
        shrink = jnp.exp2((jnp.broadcast_to(stat_ref[at, :, :1], SQUARE) - top) * SCALE)
        top_ref[at] = top
        half = BLOCK_TOKENS // 2
        before = jnp.broadcast_to(stat_ref[at, :, half : half + 1], SQUARE)
        total_ref[at] = before * shrink * (1.0 / BLOCK_TOKENS)
        sum_ref[at] = mix_ref[at] * shrink

    def mix(pair, carry):
        values = two_blocks(pool, 2 * pair, 2 * pair + 1, 1)
        for at in range(GROUP):
            weights, total = weigh(score_ref, top_ref, pair, at)
            total_ref[at] += total
            sum_ref[at] += jnp.dot(weights, values, preferred_element_type=jnp.float32)
        return carry

    lax.fori_loop(0, pairs, mix, 0)
    for at in range(GROUP):
        total = jnp.sum(total_ref[at], axis=1, keepdims=True)
        out_ref[at] = (sum_ref[at] / total).astype(out_ref.dtype)


def far_part(place, verticals, slashes, counts, query, mixed, stats, columns):
    spec = pl.BlockSpec((GROUP,) + SQUARE, lambda i: (i, 0, 0))
    return pl.pallas_call(
        far_kernel,
        out_shape=jax.ShapeDtypeStruct((SEG_BLOCKS,) + SQUARE, jnp.bfloat16),
        grid=(STEPS,),
        in_specs=scalars(4)
        + [spec] * 3
        + [pl.BlockSpec((NV, 2) + SQUARE, lambda i: (0, 0, 0, 0))],
        out_specs=spec,
        scratch_shapes=[
            pltpu.VMEM((NV // 2, GROUP, BLOCK_TOKENS, 2 * BLOCK_TOKENS), jnp.float32),
            pltpu.VMEM((GROUP,) + SQUARE, jnp.float32),
            pltpu.VMEM((GROUP,) + SQUARE, jnp.float32),
            pltpu.VMEM((GROUP,) + SQUARE, jnp.float32),
        ],
        name="far_part",
    )(place, verticals, slashes, counts, query, mixed, stats, columns)


def swapped(value, axes):
    return lax.all_to_all(value, axes, split_axis=0, concat_axis=0, tiled=True)


def shards(queries, key_row_matrix, values, verticals, slashes, counts):
    segment = lax.axis_index("seq")
    x_index = lax.axis_index("x")
    head = lax.axis_index("z") * X_CHIPS + x_index
    place = jnp.stack([segment, head, x_index]).astype(jnp.int32)

    both = packed(key_row_matrix[0], values[0])
    row = swapped(both, "z")
    hand = dealt(queries[0])
    query = swapped(hand, ("x", "z"))
    rows = [row]
    for turn in (1, 2, 3):
        rows.append(shifted(row, "x", turn, X_CHIPS, True))
    earlier = []
    for turn in range(X_CHIPS):
        earlier.append(shifted(rows[turn], "seq", 1, SEGMENTS, False))

    mine = own_columns(place, verticals, rows)
    chunk = (SEGMENTS, NV * 2 * BLOCK_TOKENS // SEGMENTS, HEAD_WIDTH)
    pieces = swapped(mine.reshape(chunk), "seq")
    piece = pieces.astype(jnp.float32).sum(0).astype(jnp.bfloat16)
    wide = jnp.broadcast_to(piece[None], chunk)
    found = swapped(wide, "seq")
    found = found.reshape((NV, 2) + SQUARE)

    mixed, stats = near_part(place, slashes, counts, query, earlier + rows)
    context = far_part(place, verticals, slashes, counts, query, mixed, stats, found)
    back = swapped(context, ("x", "z"))
    back = back.reshape((X_CHIPS, Z_CHIPS) + SQUARE).transpose(2, 1, 0, 3)
    return back.reshape(1, BLOCK_TOKENS, QUERY_HEADS * HEAD_WIDTH)


def solution(mesh):
    fine = Mesh(mesh.devices.reshape(X_CHIPS, Z_CHIPS, SEGMENTS), ("x", "z", "seq"))
    spread = P("seq", ("x", "z"), None)
    return jax.shard_map(
        shards,
        mesh=fine,
        in_specs=(spread, spread, spread, P(), P(), P()),
        out_specs=spread,
        check_vma=False,
    )
```

time: 237 us -> 216 us (0.911)
  starting transfers between devices: 53.9 us -> 40.7 us
  Pallas kernels: 30.6 us -> 23.8 us
  blocking collectives: 71.7 us -> 67.8 us
  waiting for transfers between devices: 69.7 us -> 73.4 us
    ppermute x12 -> x7, starting transfers between devices: 37.1 us -> 23.4 us  [shifted(): return lax.ppermute(value, axis, pairs)]
    all_to_all x3, waiting for transfers between devices: 28.1 us -> 38.1 us  [swapped(): return lax.all_to_all(value, axes, split_axis=0, concat_axis=0, tiled=True)]
    pallas_call x3, Pallas kernels: 25.1 us -> 18.4 us  [the longest x1 8.69 us: far_part(): pl.pallas_call(far_kernel, out_shape=jax.ShapeDtypeStruct((SEG_BLOCKS,) +...]
    ppermute x12 -> x7, waiting for transfers between devices: 41.6 us -> 35.3 us  [shifted(): return lax.ppermute(value, axis, pairs)]
    all_to_all x2, blocking collectives: 71.7 us -> 67.8 us  [swapped(): return lax.all_to_all(value, axes, split_axis=0, concat_axis=0, tiled=True)]
  transfers between devices with their start and end apart: 15 -> 10, of which waited for: 9 -> 9; matrix products, arithmetic and copies ran while one was open for 2% -> 2% of each run, Pallas kernels for 6% -> 5%
where the time goes in v2:
time: 216 us; the launch traced here: 215 us
  waiting for transfers between devices  73.4 us (34%)
  blocking collectives  67.8 us (31%)
  starting transfers between devices  40.7 us (19%)
  Pallas kernels  23.8 us (11%)
  local copies, waits for them, and re-layouts  7.66 us (4%)
    all_to_all x2, blocking collectives, swapped(): return lax.all_to_all(value, axes, split_axis=0, concat_axis=0, tiled=True)  67.8 us
    all_to_all x3, waiting for transfers between devices, swapped(): return lax.all_to_all(value, axes, split_axis=0, concat_axis=0, tiled=True)  38.1 us
    ppermute x7, waiting for transfers between devices, shifted(): return lax.ppermute(value, axis, pairs)  35.3 us
    ppermute x7, starting transfers between devices, shifted(): return lax.ppermute(value, axis, pairs)  23.4 us
    all_to_all x3, starting transfers between devices, swapped(): return lax.all_to_all(value, axes, split_axis=0, concat_axis=0, tiled=True)  17.4 us
    pallas_call x1, Pallas kernels, far_part(): pl.pallas_call(far_kernel, out_shape=jax.ShapeDtypeStruct((SEG_BLOCKS,) +...  8.69 us
    pallas_call x1, Pallas kernels, near_part(): pl.pallas_call(near_kernel, out_shape=[state, state], grid=(STEPS,), in_s...  7.31 us
  transfers between devices with their start and end apart: 10, of which 9 were waited for; matrix products, arithmetic and copies ran while one was open for 2% of the time, Pallas kernels for 5%

profile of v2, /device:TPU:16, one launch (start us, length us, event | category | flops | bytes accessed | tf_op | source)
XLA Modules:
  0.0 214.8 jit_solution(11474441017359322871)
XLA Ops:
  0.0 1.9 packed.1
  1.9 27.8 %all_to_all.25.refs_4_.refs_0_ = bf16[8,2,128,128]{3,2,1,0:T(8,128)(2,1)S(1)} all-to-all(bf16[8,2,128,128]{3,2,1,0:T(8,128)(2,1)} %packed.1), channel_id=1, replica_groups=mesh['x'=4,'z'=8,'seq'=16] {'z'}, dimensions={0} | all-to-all | bytes 1048576 | tf_op jit(solution)/shard_map/all_to_all | solution.py:328
  29.7 3.4 %collective-permute-start.1 = (bf16[8,2,128,128]{3,2,1,0:T(8,128)(2,1)S(1)}, bf16[8,2,128,128]{3,2,1,0:T(8,128)(2,1)S(1)}, u32[]{:S(2)}, u32[]{:S(2)}) collective-permute-start(bf16[8,2,128,128]{3,2,1,0:T(8,128)(2,1)S(1)} %all_to_all.25.refs_4_.refs_0_), channel_id=1, source_target_pairs={{0,128},{128,256},{256,384},{384,0},{1,129},{129,257},{257,385},{3... | collective-permute-start | bytes 1572872 | tf_op jit(solution)/shard_map/ppermute | solution.py:32
  33.1 4.6 %collective-permute-start.3 = (bf16[8,2,128,128]{3,2,1,0:T(8,128)(2,1)S(1)}, bf16[8,2,128,128]{3,2,1,0:T(8,128)(2,1)S(1)}, u32[]{:S(2)}, u32[]{:S(2)}) collective-permute-start(bf16[8,2,128,128]{3,2,1,0:T(8,128)(2,1)S(1)} %all_to_all.25.refs_4_.refs_0_), channel_id=1, source_target_pairs={{0,256},{128,384},{256,0},{384,128},{1,257},{129,385},{257,1},{385... | collective-permute-start | bytes 1572872 | tf_op jit(solution)/shard_map/ppermute | solution.py:32
  37.8 3.3 %collective-permute-start.5 = (bf16[8,2,128,128]{3,2,1,0:T(8,128)(2,1)S(1)}, bf16[8,2,128,128]{3,2,1,0:T(8,128)(2,1)S(1)}, u32[]{:S(2)}, u32[]{:S(2)}) collective-permute-start(bf16[8,2,128,128]{3,2,1,0:T(8,128)(2,1)S(1)} %all_to_all.25.refs_4_.refs_0_), channel_id=1, source_target_pairs={{0,384},{128,0},{256,128},{384,256},{1,385},{129,1},{257,129},{385... | collective-permute-start | bytes 1572872 | tf_op jit(solution)/shard_map/ppermute | solution.py:32
  41.1 0.0 copy-done.10
  41.1 0.7 copy.10.vertical_ref
  41.8 0.6 pad_add_fusion.place_ref
  42.4 4.2 %collective-permute-done.1.refs_5_.refs_1_ = bf16[8,2,128,128]{3,2,1,0:T(8,128)(2,1)S(1)} collective-permute-done((bf16[8,2,128,128]{3,2,1,0:T(8,128)(2,1)S(1)}, bf16[8,2,128,128]{3,2,1,0:T(8,128)(2,1)S(1)}, u32[]{:S(2)}, u32[]{:S(2)}) %collective-permute-start.1) | collective-permute-done | bytes 524320 | tf_op jit(solution)/shard_map/ppermute | solution.py:32
  46.6 10.4 %collective-permute-done.3.refs_6_.refs_2_ = bf16[8,2,128,128]{3,2,1,0:T(8,128)(2,1)S(1)} collective-permute-done((bf16[8,2,128,128]{3,2,1,0:T(8,128)(2,1)S(1)}, bf16[8,2,128,128]{3,2,1,0:T(8,128)(2,1)S(1)}, u32[]{:S(2)}, u32[]{:S(2)}) %collective-permute-start.3) | collective-permute-done | bytes 524320 | tf_op jit(solution)/shard_map/ppermute | solution.py:32
  57.1 1.5 collective-permute-done.5.refs_7_.refs_3_
  58.6 0.0 copy-done.1
  58.6 0.0 copy-done.3
  58.6 0.0 copy-done.5
  58.6 0.0 copy-start.7
  58.6 0.8 copy-done.7
  59.4 3.5 %own_columns.1 = bf16[6,2,128,128]{3,2,1,0:T(8,128)(2,1)} custom-call(s32[3]{0:T(128)} %pad_add_fusion.place_ref, s32[32,6]{1,0:T(8,128)} %copy.10.vertical_ref, bf16[8,2,128,128]{3,2,1,0:T(8,128)(2,1)} %copy-done.1, bf16[8,2,128,128]{3,2,1,0:T(8,128)(2,1)} %copy-done.3, bf16[8,2,128,128]{3,2,1,0:T(8,128)(2,1)} %copy-done.5, bf16[8,2,128,128]{3,2,1,0:T(8,128)(2,1)} %copy-done.7), custom_call_target="tpu_custom_call" | custom-call | tf_op jit(solution)/shard_map/own_columns/pallas_call | solution.py:94
  63.0 5.9 %all-to-all-start.2 = ((bf16[16,96,128]{2,1,0:T(8,128)(2,1)}), bf16[16,96,128]{2,1,0:T(8,128)(2,1)S(1)}, u32[]{:S(2)}, u32[]{:S(2)}) async-start(bf16[16,96,128]{2,1,0:T(8,128)(2,1)} %bitcast.12), calls=%async_computation.2 | async-start | bytes 786432 | tf_op jit(solution)/shard_map/all_to_all | solution.py:328
  68.9 2.4 %dealt.1 = bf16[32,128,128]{2,1,0:T(8,128)(2,1)} custom-call(bf16[128,4096]{1,0:T(8,128)(2,1)} %bitcast.14), custom_call_target="tpu_custom_call" | custom-call | tf_op jit(solution)/shard_map/dealt/pallas_call | solution.py:62
  71.3 0.0 copy-start.11
  71.3 0.0 copy-start.12
  71.3 9.9 %all-to-all-done.2 = bf16[16,96,128]{2,1,0:T(8,128)(2,1)S(1)} async-done(((bf16[16,96,128]{2,1,0:T(8,128)(2,1)}), bf16[16,96,128]{2,1,0:T(8,128)(2,1)S(1)}, u32[]{:S(2)}, u32[]{:S(2)}) %all-to-all-start.2) | async-done | bytes 393248 | tf_op jit(solution)/shard_map/all_to_all | solution.py:328
  81.2 6.3 %all-to-all-start = ((bf16[32,128,128]{2,1,0:T(8,128)(2,1)}), bf16[32,128,128]{2,1,0:T(8,128)(2,1)S(1)}, u32[]{:S(2)}, u32[]{:S(2)}) async-start(bf16[32,128,128]{2,1,0:T(8,128)(2,1)} %dealt.1), calls=%async_computation | async-start | bytes 2097152 | tf_op jit(solution)/shard_map/all_to_all | solution.py:328
  87.5 0.7 reduce_sum.12
  88.2 28.2 %all-to-all-done.query_ref = bf16[32,128,128]{2,1,0:T(8,128)(2,1)S(1)} async-done(((bf16[32,128,128]{2,1,0:T(8,128)(2,1)}), bf16[32,128,128]{2,1,0:T(8,128)(2,1)S(1)}, u32[]{:S(2)}, u32[]{:S(2)}) %all-to-all-start) | async-done | bytes 1048608 | tf_op jit(solution)/shard_map/all_to_all | solution.py:328
  116.4 1.6 broadcast_in_dim.2
  118.0 5.1 %all-to-all-start.3 = ((bf16[16,96,128]{2,1,0:T(8,128)(2,1)}), bf16[16,96,128]{2,1,0:T(8,128)(2,1)S(1)}, u32[]{:S(2)}, u32[]{:S(2)}) async-start(bf16[16,96,128]{2,1,0:T(8,128)(2,1)} %broadcast_in_dim.2), calls=%async_computation.3 | async-start | bytes 786432 | tf_op jit(solution)/shard_map/all_to_all | solution.py:328
  123.1 0.0 copy-done.2
  123.1 2.0 collective-permute-start
  125.1 0.0 copy-done.4
  125.1 3.4 %collective-permute-start.2 = (bf16[8,2,128,128]{3,2,1,0:T(8,128)(2,1)S(1)}, bf16[8,2,128,128]{3,2,1,0:T(8,128)(2,1)}, u32[]{:S(2)}, u32[]{:S(2)}) collective-permute-start(bf16[8,2,128,128]{3,2,1,0:T(8,128)(2,1)S(1)} %copy-done.4), channel_id=1, source_target_pairs={{0,1},{1,2},{2,3},{3,4},{4,5},{5,6},{6,7},{7,8},{8,9},{9,10},{10,1... | collective-permute-start | bytes 1572872 | tf_op jit(solution)/shard_map/ppermute | solution.py:32
  128.5 0.0 copy-done.6
  128.5 2.0 collective-permute-start.4
  130.5 4.6 %collective-permute-start.6 = (bf16[8,2,128,128]{3,2,1,0:T(8,128)(2,1)S(1)}, bf16[8,2,128,128]{3,2,1,0:T(8,128)(2,1)}, u32[]{:S(2)}, u32[]{:S(2)}) collective-permute-start(bf16[8,2,128,128]{3,2,1,0:T(8,128)(2,1)S(1)} %copy-done.8), channel_id=1, source_target_pairs={{0,1},{1,2},{2,3},{3,4},{4,5},{5,6},{6,7},{7,8},{8,9},{9,10},{10,1... | collective-permute-start | bytes 1572872 | tf_op jit(solution)/shard_map/ppermute | solution.py:32
  135.1 0.7 copy.11.slash_ref
  135.8 0.7 copy.12.count_ref
  136.5 2.2 %collective-permute-done.refs_0_ = bf16[8,2,128,128]{3,2,1,0:T(8,128)(2,1)} collective-permute-done((bf16[8,2,128,128]{3,2,1,0:T(8,128)(2,1)S(1)}, bf16[8,2,128,128]{3,2,1,0:T(8,128)(2,1)}, u32[]{:S(2)}, u32[]{:S(2)}) %collective-permute-start) | collective-permute-done | bytes 524320 | tf_op jit(solution)/shard_map/ppermute | solution.py:32
  138.8 5.6 %collective-permute-done.2.refs_1_ = bf16[8,2,128,128]{3,2,1,0:T(8,128)(2,1)} collective-permute-done((bf16[8,2,128,128]{3,2,1,0:T(8,128)(2,1)S(1)}, bf16[8,2,128,128]{3,2,1,0:T(8,128)(2,1)}, u32[]{:S(2)}, u32[]{:S(2)}) %collective-permute-start.2) | collective-permute-done | bytes 524320 | tf_op jit(solution)/shard_map/ppermute | solution.py:32
  144.4 5.6 %collective-permute-done.4.refs_2_ = bf16[8,2,128,128]{3,2,1,0:T(8,128)(2,1)} collective-permute-done((bf16[8,2,128,128]{3,2,1,0:T(8,128)(2,1)S(1)}, bf16[8,2,128,128]{3,2,1,0:T(8,128)(2,1)}, u32[]{:S(2)}, u32[]{:S(2)}) %collective-permute-start.4) | collective-permute-done | bytes 524320 | tf_op jit(solution)/shard_map/ppermute | solution.py:32
  150.0 5.6 %collective-permute-done.6.refs_3_ = bf16[8,2,128,128]{3,2,1,0:T(8,128)(2,1)} collective-permute-done((bf16[8,2,128,128]{3,2,1,0:T(8,128)(2,1)S(1)}, bf16[8,2,128,128]{3,2,1,0:T(8,128)(2,1)}, u32[]{:S(2)}, u32[]{:S(2)}) %collective-permute-start.6) | collective-permute-done | bytes 524320 | tf_op jit(solution)/shard_map/ppermute | solution.py:32
  155.6 7.3 %near_part.1 = (f32[32,128,128]{2,1,0:T(8,128)}, f32[32,128,128]{2,1,0:T(8,128)}) custom-call(s32[3]{0:T(128)} %pad_add_fusion.place_ref, s32[32,3]{1,0:T(8,128)} %copy.11.slash_ref, s32[32,2]{1,0:T(8,128)} %copy.12.count_ref, bf16[32,128,128]{2,1,0:T(8,128)(2,1)} %copy-done, bf16[8,2,128,128]{3,2,1,0:T(8,128)(2,1)} %collective-permute-done.refs_0_, ...), custom_call_target="tpu_custom_call" | custom-call | tf_op jit(solution)/shard_map/near_part/pallas_call | solution.py:224
  162.9 0.0 all-to-all-done.3
  163.0 0.0 copy-start.9
  163.0 0.8 copy-done.9
  163.7 8.7 %far_part.1 = bf16[32,128,128]{2,1,0:T(8,128)(2,1)} custom-call(s32[3]{0:T(128)} %pad_add_fusion.place_ref, s32[32,6]{1,0:T(8,128)} %copy.10.vertical_ref, s32[32,3]{1,0:T(8,128)} %copy.11.slash_ref, s32[32,2]{1,0:T(8,128)} %copy.12.count_ref, bf16[32,128,128]{2,1,0:T(8,128)(2,1)} %copy-done, f32[32,128,128]{2,1,0:T(8,128)} %get-tuple-element.7.mix_ref, ...), custom_call_target="tpu_custom_call" | custom-call | tf_op jit(solution)/shard_map/far_part/pallas_call | solution.py:309
  172.4 39.9 %all_to_all.26 = bf16[32,128,128]{2,1,0:T(8,128)(2,1)S(1)} all-to-all(bf16[32,128,128]{2,1,0:T(8,128)(2,1)} %far_part.1), channel_id=1, replica_groups=mesh['x'=4,'z'=8,'seq'=16] {'x','z'}, dimensions={0} | all-to-all | bytes 2097152 | tf_op jit(solution)/shard_map/all_to_all | solution.py:328
  212.4 0.8 copy.13
  213.2 1.6 reshape.16
  (13 shorter events, 0.0 us)
Async XLA Ops:
  0.0 41.1 %copy-start.10 = (s32[32,6]{0,1:T(8,128)S(1)}, s32[32,6]{0,1:T(8,128)}, u32[]{:S(2)}) copy-start(s32[32,6]{0,1:T(8,128)} %param.9) | copy-start | bytes 2308
  29.7 28.9 %copy-start.1 = (bf16[8,2,128,128]{3,2,1,0:T(8,128)(2,1)}, bf16[8,2,128,128]{3,2,1,0:T(8,128)(2,1)S(1)}, u32[]{:S(2)}) copy-start(bf16[8,2,128,128]{3,2,1,0:T(8,128)(2,1)S(1)} %all_to_all.25.refs_4_.refs_0_) | copy-start | bytes 1572868
  29.7 16.9 %collective-permute-start.1 = (bf16[8,2,128,128]{3,2,1,0:T(8,128)(2,1)S(1)}, bf16[8,2,128,128]{3,2,1,0:T(8,128)(2,1)S(1)}, u32[]{:S(2)}, u32[]{:S(2)}) collective-permute-start(bf16[8,2,128,128]{3,2,1,0:T(8,128)(2,1)S(1)} %all_to_all.25.refs_4_.refs_0_), channel_id=1, source_target_pairs={{0,128},{128,256},{256,384},{384,0},{1,129},{129,257},{257,385},{3... | collective-permute-start | bytes 1572872 | tf_op jit(solution)/shard_map/ppermute | solution.py:32
  33.1 23.9 %collective-permute-start.3 = (bf16[8,2,128,128]{3,2,1,0:T(8,128)(2,1)S(1)}, bf16[8,2,128,128]{3,2,1,0:T(8,128)(2,1)S(1)}, u32[]{:S(2)}, u32[]{:S(2)}) collective-permute-start(bf16[8,2,128,128]{3,2,1,0:T(8,128)(2,1)S(1)} %all_to_all.25.refs_4_.refs_0_), channel_id=1, source_target_pairs={{0,256},{128,384},{256,0},{384,128},{1,257},{129,385},{257,1},{385... | collective-permute-start | bytes 1572872 | tf_op jit(solution)/shard_map/ppermute | solution.py:32
  37.8 20.8 %collective-permute-start.5 = (bf16[8,2,128,128]{3,2,1,0:T(8,128)(2,1)S(1)}, bf16[8,2,128,128]{3,2,1,0:T(8,128)(2,1)S(1)}, u32[]{:S(2)}, u32[]{:S(2)}) collective-permute-start(bf16[8,2,128,128]{3,2,1,0:T(8,128)(2,1)S(1)} %all_to_all.25.refs_4_.refs_0_), channel_id=1, source_target_pairs={{0,384},{128,0},{256,128},{384,256},{1,385},{129,1},{257,129},{385... | collective-permute-start | bytes 1572872 | tf_op jit(solution)/shard_map/ppermute | solution.py:32
  46.6 12.0 %copy-start.3 = (bf16[8,2,128,128]{3,2,1,0:T(8,128)(2,1)}, bf16[8,2,128,128]{3,2,1,0:T(8,128)(2,1)S(1)}, u32[]{:S(2)}) copy-start(bf16[8,2,128,128]{3,2,1,0:T(8,128)(2,1)S(1)} %collective-permute-done.1.refs_5_.refs_1_) | copy-start | bytes 1572868
  57.1 1.6 copy-start.5
  58.6 0.8 copy-start.7
  63.0 18.2 %all-to-all-start.2 = ((bf16[16,96,128]{2,1,0:T(8,128)(2,1)}), bf16[16,96,128]{2,1,0:T(8,128)(2,1)S(1)}, u32[]{:S(2)}, u32[]{:S(2)}) async-start(bf16[16,96,128]{2,1,0:T(8,128)(2,1)} %bitcast.12), calls=%async_computation.2 | async-start | bytes 786432 | tf_op jit(solution)/shard_map/all_to_all | solution.py:328
  71.2 51.8 %copy-start.2 = (bf16[8,2,128,128]{3,2,1,0:T(8,128)(2,1)S(1)}, bf16[8,2,128,128]{3,2,1,0:T(8,128)(2,1)}, u32[]{:S(2)}) copy-start(bf16[8,2,128,128]{3,2,1,0:T(8,128)(2,1)} %copy-done.1) | copy-start | bytes 1572868
  71.3 53.8 %copy-start.4 = (bf16[8,2,128,128]{3,2,1,0:T(8,128)(2,1)S(1)}, bf16[8,2,128,128]{3,2,1,0:T(8,128)(2,1)}, u32[]{:S(2)}) copy-start(bf16[8,2,128,128]{3,2,1,0:T(8,128)(2,1)} %copy-done.3) | copy-start | bytes 1572868
  71.3 57.2 %copy-start.6 = (bf16[8,2,128,128]{3,2,1,0:T(8,128)(2,1)S(1)}, bf16[8,2,128,128]{3,2,1,0:T(8,128)(2,1)}, u32[]{:S(2)}) copy-start(bf16[8,2,128,128]{3,2,1,0:T(8,128)(2,1)} %copy-done.5) | copy-start | bytes 1572868
  71.3 59.3 %copy-start.8 = (bf16[8,2,128,128]{3,2,1,0:T(8,128)(2,1)S(1)}, bf16[8,2,128,128]{3,2,1,0:T(8,128)(2,1)}, u32[]{:S(2)}) copy-start(bf16[8,2,128,128]{3,2,1,0:T(8,128)(2,1)} %copy-done.7) | copy-start | bytes 1572868
  71.3 63.9 %copy-start.11 = (s32[32,3]{0,1:T(4,128)S(1)}, s32[32,3]{0,1:T(4,128)}, u32[]{:S(2)}) copy-start(s32[32,3]{0,1:T(4,128)} %param.10) | copy-start | bytes 1156
  71.3 64.6 %copy-start.12 = (s32[32,2]{0,1:T(2,128)S(1)}, s32[32,2]{0,1:T(2,128)}, u32[]{:S(2)}) copy-start(s32[32,2]{0,1:T(2,128)} %param.11) | copy-start | bytes 772
  81.2 35.2 %all-to-all-start = ((bf16[32,128,128]{2,1,0:T(8,128)(2,1)}), bf16[32,128,128]{2,1,0:T(8,128)(2,1)S(1)}, u32[]{:S(2)}, u32[]{:S(2)}) async-start(bf16[32,128,128]{2,1,0:T(8,128)(2,1)} %dealt.1), calls=%async_computation | async-start | bytes 2097152 | tf_op jit(solution)/shard_map/all_to_all | solution.py:328
  116.4 39.2 %copy-start = (bf16[32,128,128]{2,1,0:T(8,128)(2,1)}, bf16[32,128,128]{2,1,0:T(8,128)(2,1)S(1)}, u32[]{:S(2)}) copy-start(bf16[32,128,128]{2,1,0:T(8,128)(2,1)S(1)} %all-to-all-done.query_ref) | copy-start | bytes 3145732
  118.0 45.0 %all-to-all-start.3 = ((bf16[16,96,128]{2,1,0:T(8,128)(2,1)}), bf16[16,96,128]{2,1,0:T(8,128)(2,1)S(1)}, u32[]{:S(2)}, u32[]{:S(2)}) async-start(bf16[16,96,128]{2,1,0:T(8,128)(2,1)} %broadcast_in_dim.2), calls=%async_computation.3 | async-start | bytes 786432 | tf_op jit(solution)/shard_map/all_to_all | solution.py:328
  123.1 15.7 %collective-permute-start = (bf16[8,2,128,128]{3,2,1,0:T(8,128)(2,1)S(1)}, bf16[8,2,128,128]{3,2,1,0:T(8,128)(2,1)}, u32[]{:S(2)}, u32[]{:S(2)}) collective-permute-start(bf16[8,2,128,128]{3,2,1,0:T(8,128)(2,1)S(1)} %copy-done.2), channel_id=1, source_target_pairs={{0,1},{1,2},{2,3},{3,4},{4,5},{5,6},{6,7},{7,8},{8,9},{9,10},{10,1... | collective-permute-start | bytes 1572872 | tf_op jit(solution)/shard_map/ppermute | solution.py:32
  125.1 19.3 %collective-permute-start.2 = (bf16[8,2,128,128]{3,2,1,0:T(8,128)(2,1)S(1)}, bf16[8,2,128,128]{3,2,1,0:T(8,128)(2,1)}, u32[]{:S(2)}, u32[]{:S(2)}) collective-permute-start(bf16[8,2,128,128]{3,2,1,0:T(8,128)(2,1)S(1)} %copy-done.4), channel_id=1, source_target_pairs={{0,1},{1,2},{2,3},{3,4},{4,5},{5,6},{6,7},{7,8},{8,9},{9,10},{10,1... | collective-permute-start | bytes 1572872 | tf_op jit(solution)/shard_map/ppermute | solution.py:32
  128.5 21.5 %collective-permute-start.4 = (bf16[8,2,128,128]{3,2,1,0:T(8,128)(2,1)S(1)}, bf16[8,2,128,128]{3,2,1,0:T(8,128)(2,1)}, u32[]{:S(2)}, u32[]{:S(2)}) collective-permute-start(bf16[8,2,128,128]{3,2,1,0:T(8,128)(2,1)S(1)} %copy-done.6), channel_id=1, source_target_pairs={{0,1},{1,2},{2,3},{3,4},{4,5},{5,6},{6,7},{7,8},{8,9},{9,10},{10,1... | collective-permute-start | bytes 1572872 | tf_op jit(solution)/shard_map/ppermute | solution.py:32
  130.5 25.1 %collective-permute-start.6 = (bf16[8,2,128,128]{3,2,1,0:T(8,128)(2,1)S(1)}, bf16[8,2,128,128]{3,2,1,0:T(8,128)(2,1)}, u32[]{:S(2)}, u32[]{:S(2)}) collective-permute-start(bf16[8,2,128,128]{3,2,1,0:T(8,128)(2,1)S(1)} %copy-done.8), channel_id=1, source_target_pairs={{0,1},{1,2},{2,3},{3,4},{4,5},{5,6},{6,7},{7,8},{8,9},{9,10},{10,1... | collective-permute-start | bytes 1572872 | tf_op jit(solution)/shard_map/ppermute | solution.py:32
  163.0 0.8 copy-start.9
